TPU v7x, 1024 devices: a whole 8x8x8 slice. The times are simulated.
1024 devices in a mesh: boxes: 16 (over x, core), dirs: 64 (over y, z).
Axes of the slice: x: 8, y: 8, z: 8, core: 2. Of those that a mesh axis runs over, the one named last changes fastest.
Arguments:
- child_outgoing: float32 [8192, 2, 2048], P(('boxes', 'dirs')), may hold values from -6 to 6
- trans_table: float32 [316, 2, 8192], P(None, None, 'dirs'), may hold values from -0.4364358 to 0.4364358
- send_rows: int32 [16, 16, 32], replicated, may hold values from 0 to 63, as said below
- far_slot: int32 [1024, 189], P('boxes'), may hold values from 0 to 511
- far_trans: int32 [1024, 189], P('boxes'), may hold values from 0 to 315
- far_count: int32 [1024], P('boxes'), may hold values from 1 to 189, as said below
Outputs:
- child_incoming: float32 [8192, 2, 2048], P(('boxes', 'dirs'))
Inputs may be any that keep to these rules, and one draw needn't show every extreme that they name: send_rows[g, h] lists 32 distinct parents of group g, as numbers within the group, whose outgoing fields group h reads. Slot g * 32 + q of far_slot names the parent send_rows[g, h, q] for a target of group h. Entries of a parent's far lists at positions far_count and beyond are unused; some parent has 189 live entries.
All inputs are finite; a program needn't handle non-finite values.
Results may differ from a plain program's by a relative error of at most 0.0003.
Values sent between devices are 32-bit elements; how exact they have to be, the bound alone decides.
A program may use at most 32 MiB of HBM per device.

v0:
```python
import math

import jax
import jax.numpy as jnp
from jax import lax
from jax.sharding import PartitionSpec as P

TC = 32
PC = 64
TP = 64
PP = 128


shift_phase = 2.7


def interp_matrix(count_out, count_in, offset):
    target = (jnp.arange(count_out, dtype=jnp.float32) + offset) / count_out
    source = (jnp.arange(count_in, dtype=jnp.float32) + offset) / count_in
    spread = target[:, None] - source[None, :]
    orders = jnp.arange(1, count_in // 2, dtype=jnp.float32)
    series = jnp.sum(jnp.cos(2.0 * math.pi * orders[None, None, :] * spread[:, :, None]), axis=2)
    return (1.0 + 2.0 * series + jnp.cos(math.pi * count_in * spread)) / count_in


def phase_tables():
    polar = math.pi * (jnp.arange(TP, dtype=jnp.float32) + 0.5) / TP
    azimuth = 2.0 * math.pi * jnp.arange(PP, dtype=jnp.float32) / PP
    wave_x = jnp.sin(polar)[:, None] * jnp.cos(azimuth)[None, :]
    wave_y = jnp.sin(polar)[:, None] * jnp.sin(azimuth)[None, :]
    wave_z = jnp.cos(polar)[:, None] * jnp.ones((1, PP), jnp.float32)
    octant = jnp.arange(8, dtype=jnp.int32)
    sign_x = (2 * (octant % 2) - 1).astype(jnp.float32)[:, None, None]
    sign_y = (2 * (octant // 2 % 2) - 1).astype(jnp.float32)[:, None, None]
    sign_z = (2 * (octant // 4) - 1).astype(jnp.float32)[:, None, None]
    angle = shift_phase * (sign_x * wave_x + sign_y * wave_y + sign_z * wave_z)
    angle = angle.reshape(8, TP * PP)
    return (jnp.cos(angle), jnp.sin(angle))


def aggregate(child_fields):
    theta_up = interp_matrix(TP, TC, 0.5)
    phi_up = interp_matrix(PP, PC, 0.0)
    cosines, sines = phase_tables()
    fields = child_fields.reshape(-1, 2, TC, PC)
    wide_phi = jnp.einsum("bctp,jp->bctj", fields, phi_up, precision=lax.Precision.HIGHEST)
    wide = jnp.einsum("it,bctj->bcij", theta_up, wide_phi, precision=lax.Precision.HIGHEST)
    wide = wide.reshape(-1, 8, 2, TP * PP)
    real_part = wide[:, :, 0]
    imag_part = wide[:, :, 1]
    out_real = jnp.sum(cosines * real_part - sines * imag_part, axis=1)
    out_imag = jnp.sum(sines * real_part + cosines * imag_part, axis=1)
    return jnp.stack([out_real, out_imag], axis=1)


def disaggregate(parent_fields):
    theta_up = interp_matrix(TP, TC, 0.5)
    phi_up = interp_matrix(PP, PC, 0.0)
    cosines, sines = phase_tables()
    real_part = parent_fields[:, None, 0]
    imag_part = parent_fields[:, None, 1]
    turned_real = cosines * real_part + sines * imag_part
    turned_imag = cosines * imag_part - sines * real_part
    turned = jnp.stack([turned_real, turned_imag], axis=2).reshape(-1, 8, 2, TP, PP)
    narrow_theta = jnp.einsum("it,bocij->boctj", theta_up, turned, precision=lax.Precision.HIGHEST)
    narrow = jnp.einsum("boctj,jp->boctp", narrow_theta, phi_up, precision=lax.Precision.HIGHEST)
    narrow = narrow * (TC * PC / (TP * PP))
    return narrow.reshape(-1, 2, TC * PC)


def translate(source_pool, slot_index, table_index, counts, trans_table):
    group_size, far_length = slot_index.shape
    entry_block = 1
    for candidate in range(1, min(far_length, 32) + 1):
        if far_length % candidate == 0:
            entry_block = candidate
    slice_width = source_pool.shape[2]

    def one_turn(turn, total):
        start = (turn * entry_block).astype(jnp.int32)
        source_rows = lax.dynamic_slice_in_dim(slot_index, start, entry_block, 1)
        table_rows = lax.dynamic_slice_in_dim(table_index, start, entry_block, 1)
        fields = source_pool[source_rows]
        tables = trans_table[table_rows]
        live = ((start + jnp.arange(entry_block, dtype=jnp.int32))[None, :] < counts[:, None])[
            :, :, None
        ]
        field_real = fields[:, :, 0]
        field_imag = fields[:, :, 1]
        table_real = tables[:, :, 0]
        table_imag = tables[:, :, 1]
        real_sum = jnp.sum(
            jnp.where(live, field_real * table_real - field_imag * table_imag, 0.0), axis=1
        )
        imag_sum = jnp.sum(
            jnp.where(live, field_real * table_imag + field_imag * table_real, 0.0), axis=1
        )
        return total + jnp.stack([real_sum, imag_sum], axis=1)

    initial = jnp.zeros((group_size, 2, slice_width), jnp.float32)
    return lax.fori_loop(0, far_length // entry_block, one_turn, initial)


def on_device(child_outgoing, trans_table, send_rows, far_slot, far_trans, far_count):
    parent_outgoing = aggregate(child_outgoing)
    slices = lax.all_to_all(parent_outgoing, "dirs", split_axis=2, concat_axis=0, tiled=True)
    group_size = far_slot.shape[0]
    capacity = send_rows.shape[2]
    my_group = lax.axis_index("boxes")
    source_pool = lax.all_gather(slices, "boxes", axis=0, tiled=True)
    rows_map = send_rows[:, my_group, :]
    source_group = far_slot // capacity
    source_pos = far_slot % capacity
    slot_index = source_group * group_size + rows_map[source_group, source_pos]
    incoming = translate(source_pool, slot_index, far_trans, far_count, trans_table)
    returned = lax.all_to_all(incoming, "dirs", split_axis=0, concat_axis=2, tiled=True)
    return disaggregate(returned)


def solution(mesh):
    placed = (
        P(("boxes", "dirs"), None, None),
        P(None, None, "dirs"),
        P(),
        P("boxes", None),
        P("boxes", None),
        P("boxes"),
    )
    return jax.shard_map(
        on_device,
        mesh=mesh,
        in_specs=placed,
        out_specs=P(("boxes", "dirs"), None, None),
        check_vma=False,
    )
```

profile of v0, /device:TPU:2, one launch (start us, length us, event | category | flops | bytes accessed | tf_op | source)
XLA Modules:
  0.0 355.5 jit_solution(15042434511512045424)
XLA Ops:
  6.8 1.1 reshape.814
  8.0 3.3 cosine_reduce_fusion
  11.9 0.9 cosine_reduce_fusion.1
  12.8 0.8 fusion.16
  14.1 7.5 %fusion.51 = (f32[1,8,8192]{2,0,1:T(1,128)S(1)}, f32[1,8,8192]{2,0,1:T(1,128)S(1)}) fusion(f32[8192]{0:T(1024)S(1)} %broadcast_bitcast_fusion, f32[8]{0:T(128)S(1)} %get-tuple-element.188, f32[8192]{0:T(1024)S(1)} %get-tuple-element.183, f32[8]{0:T(128)S(1)} %fusion.26, f32[8192]{0:T(1024)S(1)} %get-tuple-element.182, f32[8]{0:T(128)S(1)} %get-tuple-element.189), kind=kLoop, calls=%fused_computation.117 | loop fusion | flops 393216 | bytes 622688 | tf_op jit(solution)/shard_map/cos | solution.py:38
  21.7 7.8 %subtract_reduce_fusion = (f32[8192]{0:T(1024)S(1)}, f32[8192]{0:T(1024)S(1)}) fusion(f32[1,8,8192]{2,0,1:T(1,128)S(1)} %get-tuple-element.172, f32[1,8,2,8192]{3,0,2,1:T(1,128)S(1)} %bitcast.100, f32[1,8,2,8192]{3,2,1,0:T(2,128)S(1)} %reshape.815, f32[1,8,8192]{2,0,1:T(1,128)S(1)} %get-tuple-element.173), kind=kLoop, calls=%fused_computation.28 | loop fusion | flops 507904 | bytes 1114112 | tf_op jit(solution)/shard_map/reduce_sum | solution.py:51
  29.6 6.4 %copy.45 = f32[1,2,8192]{1,0,2:T(1,128)} copy(f32[1,2,8192]{2,1,0:T(2,128)S(1)} %pad_maximum_fusion) | data formatting | bytes 131072 | tf_op jit(solution)/shard_map/stack | solution.py:53
  36.5 38.4 %reduce.2 = f32[8192,2]{1,0:T(8,128)} reduce(f32[8192,1,2]{2,1,0:T(1,128)} %bitcast.95, f32[]{:T(128)} %broadcast.989), dimensions={1}, to_apply=%bitcast.76.reduce_sub_computation | reduce | bytes 131076
  74.9 4.5 %reshape.868 = f32[64,1,256]{2,1,0:T(1,128)S(1)} reshape(f32[8192,2]{1,0:T(8,128)} %reduce.2) | data formatting | bytes 131072
  79.4 35.5 %all_to_all.36 = f32[64,1,256]{2,1,0:T(1,128)S(1)} all-to-all(f32[64,1,256]{2,1,0:T(1,128)S(1)} %reshape.868), channel_id=1, replica_groups=mesh['boxes'=16,'dirs'=64] {'dirs'}, dimensions={0} | all-to-all | bytes 131072 | tf_op jit(solution)/shard_map/all_to_all | solution.py:106
  114.9 0.8 reduce.3
  115.7 8.1 %reshape.869 = f32[8192,1,2]{2,1,0:T(1,128)} reshape(f32[64,256]{1,0:T(8,128)S(1)} %reduce.3) | data formatting | bytes 131072
  123.8 3.5 copy.46
  127.7 73.3 %gather_fusion.2 = s32[12096]{0:T(1024)S(1)} fusion(s32[16,32]{1,0:T(8,128)S(1)} %bitcast.91, s32[12096]{0:T(1024)S(1)} %reshape.835), kind=kCustom, calls=%fused_computation.2 | custom fusion | bytes 193536 | tf_op jit(solution)/shard_map/gather | solution.py:114
  201.3 127.4 %while.14 = (s32[]{:T(128)}, f32[64,2,128]{2,1,0:T(2,128)}, s32[64]{0:T(128)S(1)}, s32[64,189]{1,0:T(8,128)S(1)}, f32[1024,2,128]{2,1,0:T(2,128)}, /*index=5*/s3...) while((s32[]{:T(128)}, f32[64,2,128]{2,1,0:T(2,128)}, ...), condition=%wide.region_7.8_spmd.clone, body=%wide.region_4.7_spmd.clone.sunk | while | flops 2260834 | bytes 18715680 | solution.py:101
  201.5 5.8 %gather_fusion = f32[1728,2,128]{2,1,0:T(2,128)S(1)} fusion(f32[316,2,128]{2,1,0:T(2,128)S(1)} %get-tuple-element.273, s32[2048]{0:T(1024)S(1)} %pad_clamp_fusion.4), kind=kCustom, calls=%fused_computation.1.clone.clone.1 | custom fusion | bytes 3545856 | tf_op jit(solution)/shard_map/while/body/eval_jaxpr/gather | solution.py:84
  207.5 5.9 %gather_fusion.1 = f32[1728,2,128]{2,1,0:T(2,128)} fusion(f32[1024,2,128]{2,1,0:T(2,128)S(1)} %copy-done.2, s32[2048]{0:T(1024)S(1)} %pad_clamp_fusion.5), kind=kCustom, calls=%fused_computation.clone.clone.1 | custom fusion | bytes 3545856 | tf_op jit(solution)/shard_map/while/body/eval_jaxpr/gather | solution.py:83
  213.4 4.2 %multiply_add_fusion.4 = (f32[64,27,1,128]{3,2,1,0:T(1,128)S(1)}, f32[64,27,1,128]{3,2,1,0:T(1,128)S(1)}) fusion(f32[64,27,2,128]{3,2,1,0:T(2,128)S(1)} %bitcast.92, f32[64,27,2,128]{3,2,1,0:T(2,128)} %bitcast.93), kind=kLoop, calls=%fused_computation.7.clone.1 | loop fusion | flops 1327104 | bytes 5308416 | tf_op jit(solution)/shard_map/while/body/eval_jaxpr/add | solution.py:96
  218.1 0.7 maximum_add_fusion.2
  219.0 5.8 %gather_fusion = f32[1728,2,128]{2,1,0:T(2,128)S(1)} fusion(f32[316,2,128]{2,1,0:T(2,128)S(1)} %get-tuple-element.273, s32[2048]{0:T(1024)S(1)} %pad_clamp_fusion.4), kind=kCustom, calls=%fused_computation.1.clone.clone.1 | custom fusion | bytes 3545856 | tf_op jit(solution)/shard_map/while/body/eval_jaxpr/gather | solution.py:84
  225.0 5.9 %gather_fusion.1 = f32[1728,2,128]{2,1,0:T(2,128)} fusion(f32[1024,2,128]{2,1,0:T(2,128)S(1)} %copy-done.2, s32[2048]{0:T(1024)S(1)} %pad_clamp_fusion.5), kind=kCustom, calls=%fused_computation.clone.clone.1 | custom fusion | bytes 3545856 | tf_op jit(solution)/shard_map/while/body/eval_jaxpr/gather | solution.py:83
  230.9 4.2 %multiply_add_fusion.4 = (f32[64,27,1,128]{3,2,1,0:T(1,128)S(1)}, f32[64,27,1,128]{3,2,1,0:T(1,128)S(1)}) fusion(f32[64,27,2,128]{3,2,1,0:T(2,128)S(1)} %bitcast.92, f32[64,27,2,128]{3,2,1,0:T(2,128)} %bitcast.93), kind=kLoop, calls=%fused_computation.7.clone.1 | loop fusion | flops 1327104 | bytes 5308416 | tf_op jit(solution)/shard_map/while/body/eval_jaxpr/add | solution.py:96
  235.5 1.6 maximum_add_fusion.2
  237.3 5.8 %gather_fusion = f32[1728,2,128]{2,1,0:T(2,128)S(1)} fusion(f32[316,2,128]{2,1,0:T(2,128)S(1)} %get-tuple-element.273, s32[2048]{0:T(1024)S(1)} %pad_clamp_fusion.4), kind=kCustom, calls=%fused_computation.1.clone.clone.1 | custom fusion | bytes 3545856 | tf_op jit(solution)/shard_map/while/body/eval_jaxpr/gather | solution.py:84
  243.3 5.9 %gather_fusion.1 = f32[1728,2,128]{2,1,0:T(2,128)} fusion(f32[1024,2,128]{2,1,0:T(2,128)S(1)} %copy-done.2, s32[2048]{0:T(1024)S(1)} %pad_clamp_fusion.5), kind=kCustom, calls=%fused_computation.clone.clone.1 | custom fusion | bytes 3545856 | tf_op jit(solution)/shard_map/while/body/eval_jaxpr/gather | solution.py:83
  249.2 4.2 %multiply_add_fusion.4 = (f32[64,27,1,128]{3,2,1,0:T(1,128)S(1)}, f32[64,27,1,128]{3,2,1,0:T(1,128)S(1)}) fusion(f32[64,27,2,128]{3,2,1,0:T(2,128)S(1)} %bitcast.92, f32[64,27,2,128]{3,2,1,0:T(2,128)} %bitcast.93), kind=kLoop, calls=%fused_computation.7.clone.1 | loop fusion | flops 1327104 | bytes 5308416 | tf_op jit(solution)/shard_map/while/body/eval_jaxpr/add | solution.py:96
  253.8 1.6 maximum_add_fusion.2
  255.7 5.8 %gather_fusion = f32[1728,2,128]{2,1,0:T(2,128)S(1)} fusion(f32[316,2,128]{2,1,0:T(2,128)S(1)} %get-tuple-element.273, s32[2048]{0:T(1024)S(1)} %pad_clamp_fusion.4), kind=kCustom, calls=%fused_computation.1.clone.clone.1 | custom fusion | bytes 3545856 | tf_op jit(solution)/shard_map/while/body/eval_jaxpr/gather | solution.py:84
  261.6 5.9 %gather_fusion.1 = f32[1728,2,128]{2,1,0:T(2,128)} fusion(f32[1024,2,128]{2,1,0:T(2,128)S(1)} %copy-done.2, s32[2048]{0:T(1024)S(1)} %pad_clamp_fusion.5), kind=kCustom, calls=%fused_computation.clone.clone.1 | custom fusion | bytes 3545856 | tf_op jit(solution)/shard_map/while/body/eval_jaxpr/gather | solution.py:83
  267.5 4.2 %multiply_add_fusion.4 = (f32[64,27,1,128]{3,2,1,0:T(1,128)S(1)}, f32[64,27,1,128]{3,2,1,0:T(1,128)S(1)}) fusion(f32[64,27,2,128]{3,2,1,0:T(2,128)S(1)} %bitcast.92, f32[64,27,2,128]{3,2,1,0:T(2,128)} %bitcast.93), kind=kLoop, calls=%fused_computation.7.clone.1 | loop fusion | flops 1327104 | bytes 5308416 | tf_op jit(solution)/shard_map/while/body/eval_jaxpr/add | solution.py:96
  272.2 1.6 maximum_add_fusion.2
  274.0 5.8 %gather_fusion = f32[1728,2,128]{2,1,0:T(2,128)S(1)} fusion(f32[316,2,128]{2,1,0:T(2,128)S(1)} %get-tuple-element.273, s32[2048]{0:T(1024)S(1)} %pad_clamp_fusion.4), kind=kCustom, calls=%fused_computation.1.clone.clone.1 | custom fusion | bytes 3545856 | tf_op jit(solution)/shard_map/while/body/eval_jaxpr/gather | solution.py:84
  280.0 5.9 %gather_fusion.1 = f32[1728,2,128]{2,1,0:T(2,128)} fusion(f32[1024,2,128]{2,1,0:T(2,128)S(1)} %copy-done.2, s32[2048]{0:T(1024)S(1)} %pad_clamp_fusion.5), kind=kCustom, calls=%fused_computation.clone.clone.1 | custom fusion | bytes 3545856 | tf_op jit(solution)/shard_map/while/body/eval_jaxpr/gather | solution.py:83
  285.8 4.2 %multiply_add_fusion.4 = (f32[64,27,1,128]{3,2,1,0:T(1,128)S(1)}, f32[64,27,1,128]{3,2,1,0:T(1,128)S(1)}) fusion(f32[64,27,2,128]{3,2,1,0:T(2,128)S(1)} %bitcast.92, f32[64,27,2,128]{3,2,1,0:T(2,128)} %bitcast.93), kind=kLoop, calls=%fused_computation.7.clone.1 | loop fusion | flops 1327104 | bytes 5308416 | tf_op jit(solution)/shard_map/while/body/eval_jaxpr/add | solution.py:96
  290.5 1.6 maximum_add_fusion.2
  292.3 5.8 %gather_fusion = f32[1728,2,128]{2,1,0:T(2,128)S(1)} fusion(f32[316,2,128]{2,1,0:T(2,128)S(1)} %get-tuple-element.273, s32[2048]{0:T(1024)S(1)} %pad_clamp_fusion.4), kind=kCustom, calls=%fused_computation.1.clone.clone.1 | custom fusion | bytes 3545856 | tf_op jit(solution)/shard_map/while/body/eval_jaxpr/gather | solution.py:84
  298.3 5.9 %gather_fusion.1 = f32[1728,2,128]{2,1,0:T(2,128)} fusion(f32[1024,2,128]{2,1,0:T(2,128)S(1)} %copy-done.2, s32[2048]{0:T(1024)S(1)} %pad_clamp_fusion.5), kind=kCustom, calls=%fused_computation.clone.clone.1 | custom fusion | bytes 3545856 | tf_op jit(solution)/shard_map/while/body/eval_jaxpr/gather | solution.py:83
  304.1 4.2 %multiply_add_fusion.4 = (f32[64,27,1,128]{3,2,1,0:T(1,128)S(1)}, f32[64,27,1,128]{3,2,1,0:T(1,128)S(1)}) fusion(f32[64,27,2,128]{3,2,1,0:T(2,128)S(1)} %bitcast.92, f32[64,27,2,128]{3,2,1,0:T(2,128)} %bitcast.93), kind=kLoop, calls=%fused_computation.7.clone.1 | loop fusion | flops 1327104 | bytes 5308416 | tf_op jit(solution)/shard_map/while/body/eval_jaxpr/add | solution.py:96
  308.8 1.6 maximum_add_fusion.2
  310.6 5.8 %gather_fusion = f32[1728,2,128]{2,1,0:T(2,128)S(1)} fusion(f32[316,2,128]{2,1,0:T(2,128)S(1)} %get-tuple-element.273, s32[2048]{0:T(1024)S(1)} %pad_clamp_fusion.4), kind=kCustom, calls=%fused_computation.1.clone.clone.1 | custom fusion | bytes 3545856 | tf_op jit(solution)/shard_map/while/body/eval_jaxpr/gather | solution.py:84
  316.6 5.9 %gather_fusion.1 = f32[1728,2,128]{2,1,0:T(2,128)} fusion(f32[1024,2,128]{2,1,0:T(2,128)S(1)} %copy-done.2, s32[2048]{0:T(1024)S(1)} %pad_clamp_fusion.5), kind=kCustom, calls=%fused_computation.clone.clone.1 | custom fusion | bytes 3545856 | tf_op jit(solution)/shard_map/while/body/eval_jaxpr/gather | solution.py:83
  322.5 4.2 %multiply_add_fusion.4 = (f32[64,27,1,128]{3,2,1,0:T(1,128)S(1)}, f32[64,27,1,128]{3,2,1,0:T(1,128)S(1)}) fusion(f32[64,27,2,128]{3,2,1,0:T(2,128)S(1)} %bitcast.92, f32[64,27,2,128]{3,2,1,0:T(2,128)} %bitcast.93), kind=kLoop, calls=%fused_computation.7.clone.1 | loop fusion | flops 1327104 | bytes 5308416 | tf_op jit(solution)/shard_map/while/body/eval_jaxpr/add | solution.py:96
  327.1 1.6 maximum_add_fusion.2
  328.7 4.6 %all-to-all-start.1 = ((f32[64,2,128]{2,1,0:T(2,128)}), f32[64,2,128]{2,1,0:T(2,128)S(1)}, u32[]{:S(2)}, u32[]{:S(2)}) async-start(f32[64,2,128]{2,1,0:T(2,128)} %get-tuple-element.129), calls=%async_computation.1 | async-start | bytes 131072 | tf_op jit(solution)/shard_map/all_to_all | solution.py:116
  333.4 12.2 %all-to-all-done.1 = f32[64,2,128]{2,1,0:T(2,128)S(1)} async-done(((f32[64,2,128]{2,1,0:T(2,128)}), f32[64,2,128]{2,1,0:T(2,128)S(1)}, u32[]{:S(2)}, u32[]{:S(2)}) %all-to-all-start.1) | async-done | bytes 65568 | tf_op jit(solution)/shard_map/all_to_all | solution.py:116
  345.6 1.1 multiply_add_fusion.1
  346.7 0.6 convolution_bitcast_fusion
  347.8 0.8 reshape.818
  (112 shorter events, 8.5 us)
Async XLA Ops:
  6.5 121.1 %copy-start = (s32[16,16,32]{2,1,0:T(8,128)S(1)}, s32[16,16,32]{2,1,0:T(8,128)}, u32[]{:S(2)}) copy-start(s32[16,16,32]{2,1,0:T(8,128)} %param.10) | copy-start | bytes 98308
  6.5 194.7 %all-gather.3.cloned.1.call-start = ((), (), s32[]{:S(2)}) async-start(), calls=%async_computation.2 | async-start | bytes 1114112 | tf_op jit(solution)/shard_map/all_gather | solution.py:110
  115.7 11.6 %copy-start.4 = (s32[64,189]{1,0:T(8,128)S(1)}, s32[64,189]{1,0:T(8,128)}, u32[]{:S(2)}) copy-start(s32[64,189]{1,0:T(8,128)} %param.11) | copy-start | bytes 145156
  127.7 73.6 %copy-start.1 = (f32[316,2,128]{2,1,0:T(2,128)S(1)}, f32[316,2,128]{2,1,0:T(2,128)}, u32[]{:S(2)}) copy-start(f32[316,2,128]{2,1,0:T(2,128)} %param.9) | copy-start | bytes 970756
  127.7 73.6 %copy-start.3 = (s32[64,189]{1,0:T(8,128)S(1)}, s32[64,189]{1,0:T(8,128)}, u32[]{:S(2)}) copy-start(s32[64,189]{1,0:T(8,128)} %param.12) | copy-start | bytes 145156
  127.7 73.6 %copy-start.5 = (s32[64]{0:T(128)S(1)}, s32[64]{0:T(128)}, u32[]{:S(2)}) copy-start(s32[64]{0:T(128)} %param.13) | copy-start | bytes 772
  201.3 6.2 %copy-start.2 = (f32[1024,2,128]{2,1,0:T(2,128)S(1)}, f32[1024,2,128]{2,1,0:T(2,128)}, u32[]{:S(2)}) copy-start(f32[1024,2,128]{2,1,0:T(2,128)} %get-tuple-element.271) | copy-start | bytes 3145732 | tf_op jit(solution)/shard_map/while
  218.8 6.2 %copy-start.2 = (f32[1024,2,128]{2,1,0:T(2,128)S(1)}, f32[1024,2,128]{2,1,0:T(2,128)}, u32[]{:S(2)}) copy-start(f32[1024,2,128]{2,1,0:T(2,128)} %get-tuple-element.271) | copy-start | bytes 3145732 | tf_op jit(solution)/shard_map/while
  237.1 6.2 %copy-start.2 = (f32[1024,2,128]{2,1,0:T(2,128)S(1)}, f32[1024,2,128]{2,1,0:T(2,128)}, u32[]{:S(2)}) copy-start(f32[1024,2,128]{2,1,0:T(2,128)} %get-tuple-element.271) | copy-start | bytes 3145732 | tf_op jit(solution)/shard_map/while
  255.4 6.2 %copy-start.2 = (f32[1024,2,128]{2,1,0:T(2,128)S(1)}, f32[1024,2,128]{2,1,0:T(2,128)}, u32[]{:S(2)}) copy-start(f32[1024,2,128]{2,1,0:T(2,128)} %get-tuple-element.271) | copy-start | bytes 3145732 | tf_op jit(solution)/shard_map/while
  273.7 6.2 %copy-start.2 = (f32[1024,2,128]{2,1,0:T(2,128)S(1)}, f32[1024,2,128]{2,1,0:T(2,128)}, u32[]{:S(2)}) copy-start(f32[1024,2,128]{2,1,0:T(2,128)} %get-tuple-element.271) | copy-start | bytes 3145732 | tf_op jit(solution)/shard_map/while
  292.0 6.2 %copy-start.2 = (f32[1024,2,128]{2,1,0:T(2,128)S(1)}, f32[1024,2,128]{2,1,0:T(2,128)}, u32[]{:S(2)}) copy-start(f32[1024,2,128]{2,1,0:T(2,128)} %get-tuple-element.271) | copy-start | bytes 3145732 | tf_op jit(solution)/shard_map/while
  310.3 6.2 %copy-start.2 = (f32[1024,2,128]{2,1,0:T(2,128)S(1)}, f32[1024,2,128]{2,1,0:T(2,128)}, u32[]{:S(2)}) copy-start(f32[1024,2,128]{2,1,0:T(2,128)} %get-tuple-element.271) | copy-start | bytes 3145732 | tf_op jit(solution)/shard_map/while
  328.7 16.9 %all-to-all-start.1 = ((f32[64,2,128]{2,1,0:T(2,128)}), f32[64,2,128]{2,1,0:T(2,128)S(1)}, u32[]{:S(2)}, u32[]{:S(2)}) async-start(f32[64,2,128]{2,1,0:T(2,128)} %get-tuple-element.129), calls=%async_computation.1 | async-start | bytes 131072 | tf_op jit(solution)/shard_map/all_to_all | solution.py:116
Sparse Core Ops, SparseCore 0:
  127.4 34.6 all-gather.2
where the time goes:
time: 356 us; the launch traced here: 355 us
  local copies, waits for them, and re-layouts  183 us (51%)
  other arithmetic  104 us (29%)
  blocking collectives  35.5 us (10%)
  between operations  13.7 us (4%)
  waiting for transfers between devices  12.2 us (3%)
  starting transfers between devices  4.62 us (1%)
    gather x2, local copies, waits for them, and re-layouts, on_device(): slot_index = source_group * group_size + rows_map[source_group, source_pos]  73.5 us
    gather x7, local copies, waits for them, and re-layouts, one_turn(): fields = source_pool[source_rows]  41.1 us
    gather x7, local copies, waits for them, and re-layouts, one_turn(): tables = trans_table[table_rows]  40.7 us
    unnamed x2, other arithmetic  38.4 us
    all_to_all x1, blocking collectives, on_device(): lax.all_to_all(parent_outgoing, 'dirs', split_axis=2, concat_axis=0, tile...  35.5 us
    add x7, other arithmetic, one_turn(): field_real * table_imag + field_imag * table_real  29.7 us
    unnamed x13, local copies, waits for them, and re-layouts  13.1 us
    all_to_all x1, waiting for transfers between devices, on_device(): lax.all_to_all(incoming, 'dirs', split_axis=0, concat_axis=2, tiled=True)  12.2 us
  transfers between devices with their start and end apart: 2, of which 1 were waited for; matrix products, arithmetic and copies ran while one was open for 21% of the time, Pallas kernels for 0%

commit v1 on v0

v1 whole, which is shorter than its diff:
```python
import functools
import math

import jax
import jax.numpy as jnp
import numpy as np
from jax import lax
from jax.experimental import pallas as pl
from jax.experimental.pallas import tpu as pltpu
from jax.sharding import PartitionSpec as P

TC = 32
PC = 64
TP = 64
PP = 128
NTRANS = 316
NFAR = 189
CAP = 32
GROUPS = 16
SHIFT_PHASE = 2.7

NX = 8
NY = 8
NZ = 8
BF = jnp.bfloat16
MESH = pl.DeviceIdType.MESH


def interp_matrix(count_out, count_in, offset):
    target = (np.arange(count_out) + offset) / count_out
    source = (np.arange(count_in) + offset) / count_in
    spread = target[:, None] - source[None, :]
    orders = np.arange(1, count_in // 2)
    series = np.sum(np.cos(2.0 * math.pi * orders[None, None, :] * spread[:, :, None]), axis=2)
    return (1.0 + 2.0 * series + np.cos(math.pi * count_in * spread)) / count_in


def phase_tables():
    polar = math.pi * (np.arange(TP) + 0.5) / TP
    azimuth = 2.0 * math.pi * np.arange(PP) / PP
    wave_x = np.sin(polar)[:, None] * np.cos(azimuth)[None, :]
    wave_y = np.sin(polar)[:, None] * np.sin(azimuth)[None, :]
    wave_z = np.cos(polar)[:, None] * np.ones((1, PP))
    octant = np.arange(8)
    sign_x = (2 * (octant % 2) - 1)[:, None, None]
    sign_y = (2 * (octant // 2 % 2) - 1)[:, None, None]
    sign_z = (2 * (octant // 4) - 1)[:, None, None]
    angle = SHIFT_PHASE * (sign_x * wave_x + sign_y * wave_y + sign_z * wave_z)
    return np.cos(angle), np.sin(angle)


def halves(matrix):
    high = np.asarray(matrix, np.float32).astype(BF)
    low = (np.asarray(matrix, np.float32) - high.astype(np.float32)).astype(BF)
    return high, low


def constants():
    theta = interp_matrix(TP, TC, 0.5)
    phi = interp_matrix(PP, PC, 0.0)
    cosines, sines = phase_tables()
    pair = np.zeros((128, 256))
    pair[:64, :128] = phi.T
    pair[64:, 128:] = phi.T
    high, low = halves(pair)
    phi_out = np.concatenate([high, high, low], axis=0)
    theta_ba = np.concatenate([theta[:, 0::2], theta[:, 1::2]], axis=1)
    high, low = halves(theta_ba)
    theta_out = np.concatenate([high, high, low], axis=1)
    order = np.arange(64).reshape(8, 8).T.reshape(-1)
    high, low = halves(theta_ba.T[:, order])
    theta_in = np.concatenate([high, high, low], axis=1)
    back = np.zeros((256, 128))
    back[:128, :64] = phi
    back[128:, 64:] = phi
    high, low = halves(back * (TC * PC / (TP * PP)))
    phi_in = np.concatenate([high, high, low], axis=0)
    f32 = np.float32
    return dict(
        phi_out=phi_out, theta_out=theta_out, cos_out=cosines.astype(f32), sin_out=sines.astype(f32),
        theta_in=theta_in, phi_in=phi_in, cos_in=cosines[:, order].astype(f32), sin_in=sines[:, order].astype(f32),
    )


def split(value):
    high = value.astype(BF)
    low = (value - high.astype(jnp.float32)).astype(BF)
    return high, low


def position():
    b = lax.axis_index("boxes")
    d = lax.axis_index("dirs")
    return b, b // 2, b % 2, d // NZ, d % NZ


def signal(barrier, device):
    pl.semaphore_signal(barrier, inc=1, device_id=device, device_id_type=MESH)


def exchange(send0, recv1, send2, last, sems, b, y, z):
    ssem1, rsem1, ssem2, rsem2 = sems

    def along_y(k, peer_slot):
        target = (y + k) % NY
        return pltpu.make_async_remote_copy(
            src_ref=send0.at[pl.ds(pl.multiple_of(target * 16, 16), 16)],
            dst_ref=recv1.at[pl.ds(pl.multiple_of(peer_slot * 16, 16), 16)],
            send_sem=ssem1.at[k - 1], recv_sem=rsem1.at[k - 1],
            device_id=(b, target * NZ + z), device_id_type=MESH)

    for k in range(1, NY):
        along_y(k, y).start()
    mine = pl.ds(pl.multiple_of(y * 16, 16), 16)
    recv1[mine, :] = send0[mine, :]
    for k in range(1, NY):
        along_y(k, (y + NY - k) % NY).wait_recv()
    for target in range(NZ):
        for r in range(2):
            send2[target, r] = recv1[pl.ds(r * 8 + target, 8, stride=16), :]

    def along_z(k, peer_slot):
        target = (z + k) % NZ
        return pltpu.make_async_remote_copy(
            src_ref=send2.at[target], dst_ref=last.at[peer_slot],
            send_sem=ssem2.at[k - 1], recv_sem=rsem2.at[k - 1],
            device_id=(b, y * NZ + target), device_id_type=MESH)

    for k in range(1, NZ):
        along_z(k, z).start()
    last[z] = send2[z]
    for k in range(1, NZ):
        along_z(k, (z + NZ - k) % NZ).wait_recv()

    def drain():
        for k in range(1, NY):
            along_y(k, y).wait_send()
        for k in range(1, NZ):
            along_z(k, z).wait_send()
    return drain


def out_kernel(x_ref, phi_ref, theta_ref, cos_ref, sin_ref, pool_ref,
               wide_phi, send0, recv1, send2, ssem1, rsem1, ssem2, rsem2, ssem3, rsem3, ssem4, rsem4):
    b, x, core, y, z = position()
    barrier = pltpu.get_barrier_semaphore()
    for k in range(1, NY):
        signal(barrier, (b, (y + k) % NY * NZ + z))
    for k in range(1, NZ):
        signal(barrier, (b, y * NZ + (z + k) % NZ))
    d = y * NZ + z
    right = (x + 1) % NX * 2 + core
    left = (x + NX - 1) % NX * 2 + core
    other = x * 2 + 1 - core
    for device in (right, left, other):
        signal(barrier, (device, d))

    high, low = split(x_ref[...])
    both = jnp.dot(jnp.concatenate([high, low, high], axis=1), phi_ref[...],
                   preferred_element_type=jnp.float32)
    wide_phi[:256, :] = both[:, :128]
    wide_phi[256:, :] = both[:, 128:]
    real = jnp.zeros((TP, PP), jnp.float32)
    imag = jnp.zeros((TP, PP), jnp.float32)
    for o in range(8):
        parts = []
        for r in range(2):
            parts.append(jnp.concatenate(
                [wide_phi[pl.ds(half * 256 + o * 32 + r, 16, stride=2), :] for half in range(2)], axis=0))
        high, low = split(jnp.concatenate(parts, axis=1))
        wide = jnp.dot(theta_ref[...], jnp.concatenate([high, low, high], axis=0),
                       preferred_element_type=jnp.float32)
        cosine, sine = cos_ref[o], sin_ref[o]
        real += cosine * wide[:, :128] - sine * wide[:, 128:]
        imag += sine * wide[:, :128] + cosine * wide[:, 128:]
    for i in range(NY):
        send0[i * 16:i * 16 + 8, :] = real[i * 8:i * 8 + 8]
        send0[i * 16 + 8:i * 16 + 16, :] = imag[i * 8:i * 8 + 8]

    pl.semaphore_wait(barrier, NY + NZ - 2 + 3)
    drain = exchange(send0, recv1, send2, pool_ref.at[b], (ssem1, rsem1, ssem2, rsem2), b, y, z)

    def part(h):
        return pl.ds(h * 4, 4)

    steps = [(s, h) for s in range(3) for h in range(2)]
    slots = steps + [(3, 0)]

    def ring(way, n, sent):
        s, h = slots[n]
        h = way if s == 3 else h
        back = s if sent else s + 1
        origin = (x + NX - back) % NX if way == 0 else (x + back) % NX
        block = pool_ref.at[origin * 2 + core, part(h)]
        return pltpu.make_async_remote_copy(
            src_ref=block, dst_ref=block, send_sem=ssem3.at[way, n], recv_sem=rsem3.at[way, n],
            device_id=((right, left)[way], d), device_id_type=MESH), origin, h

    def across(n, origin, h, mine):
        block = pool_ref.at[origin * 2 + (core if mine else 1 - core), part(h)]
        return pltpu.make_async_remote_copy(
            src_ref=block, dst_ref=block, send_sem=ssem4.at[n], recv_sem=rsem4.at[n],
            device_id=(other, d), device_id_type=MESH)

    crossed = []
    for n in range(2):
        ring(0, n, True)[0].start()
        ring(1, n, True)[0].start()
    for h in range(2):
        across(len(crossed), x, h, True).start()
        crossed.append((x, h))
    for n in range(7):
        for way in range(2):
            copy, origin, h = ring(way, n, False)
            copy.wait_recv()
            s, half = slots[n]
            if s < 2 or (s == 2 and half == way):
                after = slots.index((s + 1, half)) if s < 2 else 6
                ring(way, after, True)[0].start()
            across(len(crossed), origin, h, True).start()
            crossed.append((origin, h))
    for n, (origin, h) in enumerate(crossed):
        across(n, origin, h, False).wait_recv()
    drain()
    for n in range(7):
        for way in range(2):
            ring(way, n, True)[0].wait_send()
    for n, (origin, h) in enumerate(crossed):
        across(n, origin, h, True).wait_send()


def translate_kernel(count_hbm, slot_hbm, trans_hbm, rows_ref, pool_ref, table_ref, out_ref,
                     source4, slots4, table4, acc, count_ref, slot_ref, trans_ref, sems):
    copies = [pltpu.make_async_copy(src, dst, sems.at[i]) for i, (src, dst) in enumerate(
        [(count_hbm, count_ref), (slot_hbm, slot_ref), (trans_hbm, trans_ref)])]
    for copy in copies:
        copy.start()
    for v in range(0, NTRANS, 8):
        n = min(8, NTRANS - v)
        for r in range(2):
            rows = table_ref[pl.ds(v * 2 + r, n, stride=2), :]
            table4[pl.ds(v * 4 + 2 * r, n, stride=4), :] = rows
            table4[pl.ds(v * 4 + 2 * r + 1, n, stride=4), :] = rows
    for i in range(GROUPS * 8):
        for r in range(2):
            rows = pool_ref[i * 16 + r * 8:i * 16 + r * 8 + 8, :]
            source4[pl.ds(i * 32 + r, 8, stride=4), :] = rows
            source4[pl.ds(i * 32 + r + 2, 8, stride=4), :] = rows

    def pick(i, carry):
        for j in range(8):
            s = i * 8 + j
            m = rows_ref[s]
            row = s // CAP * 64 + m % 8 * 8 + m // 8
            slots4[s] = source4[pl.ds(pl.multiple_of(row * 4, 4), 4), :]
        return carry

    lax.fori_loop(0, GROUPS * CAP // 8, pick, 0)
    for copy in copies:
        copy.wait()

    def one_target(t, carry):
        count = count_ref[t]

        def turn(width, base, limit, sums):
            sums = list(sums)
            for j in range(width):
                e = base + j
                value = slots4[slot_ref[t, e]] * table4[pl.ds(pl.multiple_of(trans_ref[t, e] * 4, 4), 4), :]
                if limit is not None:
                    value = jnp.where(e < limit, value, 0.0)
                sums[j % 4] = sums[j % 4] + value
            return tuple(sums)

        zero = jnp.zeros((4, 128), jnp.float32)
        wide = count // 32
        sums = lax.fori_loop(0, wide, lambda i, c: turn(32, i * 32, None, c), (zero,) * 4)
        base = wide * 32
        full = (count - base) // 8
        sums = lax.fori_loop(0, full, lambda i, c: turn(8, base + i * 8, None, c), sums)
        base = base + full * 8

        def single(e, c):
            return (c[0] + slots4[slot_ref[t, e]] * table4[pl.ds(pl.multiple_of(trans_ref[t, e] * 4, 4), 4), :],) + c[1:]
        sums = lax.fori_loop(base, count, single, sums)
        acc[t] = (sums[0] + sums[1]) + (sums[2] + sums[3])
        return carry

    lax.fori_loop(0, 64, one_target, 0)
    for i in range(8):
        q = [acc[i * 8:i * 8 + 8, k, :] for k in range(4)]
        out_ref[i * 16:i * 16 + 8, :] = q[0] - q[3]
        out_ref[i * 16 + 8:i * 16 + 16, :] = q[1] + q[2]


def in_kernel(field_ref, phi_ref, theta_ref, cos_ref, sin_ref, out_ref,
              recv1, send2, last, ssem1, rsem1, ssem2, rsem2):
    b, x, core, y, z = position()
    barrier = pltpu.get_barrier_semaphore()
    for k in range(1, NY):
        signal(barrier, (b, (y + k) % NY * NZ + z))
    for k in range(1, NZ):
        signal(barrier, (b, y * NZ + (z + k) % NZ))
    pl.semaphore_wait(barrier, NY + NZ - 2)
    drain = exchange(field_ref, recv1, send2, last, (ssem1, rsem1, ssem2, rsem2), b, y, z)
    real = last[:, 0].reshape(TP, PP)
    imag = last[:, 1].reshape(TP, PP)
    narrow = []
    for o in range(8):
        cosine, sine = cos_ref[o], sin_ref[o]
        high, low = split(jnp.concatenate([cosine * real + sine * imag, cosine * imag - sine * real], axis=1))
        rows = jnp.dot(theta_ref[...], jnp.concatenate([high, low, high], axis=0),
                       preferred_element_type=jnp.float32)
        for r in range(2):
            cols = rows[:, r * 128:(r + 1) * 128]
            narrow.append(jnp.concatenate([cols[:16], cols[16:]], axis=1))
    high, low = split(jnp.concatenate(narrow, axis=0))
    result = jnp.dot(jnp.concatenate([high, low, high], axis=1), phi_ref[...],
                     preferred_element_type=jnp.float32)
    for o in range(8):
        for r in range(2):
            n = o * 2 + r
            out_ref[pl.ds(o * 32 + r, 16, stride=2), :] = result[n * 16:(n + 1) * 16]
    drain()


def whole():
    return pl.BlockSpec(memory_space=pltpu.VMEM)


def dma(*shape):
    return pltpu.SemaphoreType.DMA(shape)


def outgoing_pool(fields, const):
    f32 = jnp.float32
    return pl.pallas_call(
        out_kernel,
        out_shape=jax.ShapeDtypeStruct((GROUPS, NZ, 2, NY, 128), f32),
        in_specs=[whole()] * 5, out_specs=whole(),
        scratch_shapes=[pltpu.VMEM((512, 128), f32), pltpu.VMEM((128, 128), f32), pltpu.VMEM((128, 128), f32),
                        pltpu.VMEM((NZ, 2, NY, 128), f32),
                        dma(7), dma(7), dma(7), dma(7), dma(2, 7), dma(2, 7), dma(16), dma(16)],
        compiler_params=pltpu.CompilerParams(collective_id=0, has_side_effects=True, vmem_limit_bytes=32 << 20),
        name="outgoing",
    )(fields, const["phi_out"], const["theta_out"], const["cos_out"], const["sin_out"])


def translate(counts, slots, trans, rows, pool, table):
    f32 = jnp.float32
    smem = pl.BlockSpec(memory_space=pltpu.SMEM)
    raw = pl.BlockSpec(memory_space=pl.ANY)
    return pl.pallas_call(
        translate_kernel,
        out_shape=jax.ShapeDtypeStruct((128, 128), f32),
        in_specs=[raw, raw, raw, smem, whole(), whole()], out_specs=whole(),
        scratch_shapes=[pltpu.VMEM((GROUPS * 64 * 4, 128), f32), pltpu.VMEM((GROUPS * CAP, 4, 128), f32),
                        pltpu.VMEM((NTRANS * 4, 128), f32), pltpu.VMEM((64, 4, 128), f32),
                        pltpu.SMEM((64,), jnp.int32), pltpu.SMEM((64, NFAR), jnp.int32),
                        pltpu.SMEM((64, NFAR), jnp.int32), dma(3)],
        compiler_params=pltpu.CompilerParams(vmem_limit_bytes=32 << 20),
        name="translate",
    )(counts, slots, trans, rows, pool, table)


def incoming_fields(field, const):
    f32 = jnp.float32
    return pl.pallas_call(
        in_kernel,
        out_shape=jax.ShapeDtypeStruct((256, 128), f32),
        in_specs=[whole()] * 5, out_specs=whole(),
        scratch_shapes=[pltpu.VMEM((128, 128), f32), pltpu.VMEM((NZ, 2, NY, 128), f32), pltpu.VMEM((NZ, 2, NY, 128), f32),
                        dma(7), dma(7), dma(7), dma(7)],
        compiler_params=pltpu.CompilerParams(collective_id=1, has_side_effects=True, vmem_limit_bytes=32 << 20),
        name="incoming",
    )(field, const["phi_in"], const["theta_in"], const["cos_in"], const["sin_in"])


def on_device(const, child_outgoing, trans_table, send_rows, far_slot, far_trans, far_count):
    fields = child_outgoing.reshape(8, 2, 16, 128).transpose(0, 2, 1, 3).reshape(256, 128)
    pool = outgoing_pool(fields, const)
    rows = lax.dynamic_index_in_dim(send_rows, lax.axis_index("boxes"), 1, keepdims=False).reshape(GROUPS * CAP)
    field = translate(far_count, far_slot, far_trans, rows, pool.reshape(GROUPS * 128, 128),
                      trans_table.reshape(NTRANS * 2, 128))
    out = incoming_fields(field, const)
    return out.reshape(8, 16, 2, 128).transpose(0, 2, 1, 3).reshape(8, 2, 2048)


def solution(mesh):
    placed = (
        P(("boxes", "dirs"), None, None),
        P(None, None, "dirs"),
        P(),
        P("boxes", None),
        P("boxes", None),
        P("boxes"),
    )
    const = {name: np.asarray(value) for name, value in constants().items()}
    return jax.shard_map(
        functools.partial(on_device, const),
        mesh=mesh,
        in_specs=placed,
        out_specs=P(("boxes", "dirs"), None, None),
        check_vma=False,
    )
```

time: 356 us -> 110 us (0.31)
  local copies, waits for them, and re-layouts: 183 us -> 6.05 us
  other arithmetic: 104 us -> 0 us
  Pallas kernels: 0 us -> 103 us
  blocking collectives: 35.5 us -> 0 us
  between operations: 13.7 us -> 0.1 us
  waiting for transfers between devices: 12.2 us -> 0 us
  starting transfers between devices: 4.62 us -> 0 us
    gather x16 -> x0, local copies, waits for them, and re-layouts: 155 us -> none  [the longest x2 73.5 us: on_device(): slot_index = source_group * group_size + rows_map[source_group, source_pos]]
    pallas_call x0 -> x3, Pallas kernels: none -> 103 us  [the longest x1 46.4 us: outgoing_pool(): pl.pallas_call(out_kernel, out_shape=jax.ShapeDtypeStruct((GROUPS, NZ, 2,...]
    add x23 -> x0, other arithmetic: 40.9 us -> none  [the longest x7 29.7 us: one_turn(): field_real * table_imag + field_imag * table_real]
    unnamed x2 -> x0, other arithmetic: 38.4 us -> none
    all_to_all x1 -> x0, blocking collectives: 35.5 us -> none  [on_device(): lax.all_to_all(parent_outgoing, 'dirs', split_axis=2, concat_axis=0, tile...]
    reduce_sum x10 -> x0, other arithmetic: 14.2 us -> none  [the longest x1 7.84 us: aggregate(): out_real = jnp.sum(cosines * real_part - sines * imag_part, axis=1)]
    all_to_all x1 -> x0, waiting for transfers between devices: 12.2 us -> none  [on_device(): lax.all_to_all(incoming, 'dirs', split_axis=0, concat_axis=2, tiled=True)]
    cos x2 -> x0, other arithmetic: 7.6 us -> none  [the longest x1 7.55 us: phase_tables(): return (jnp.cos(angle), jnp.sin(angle))]
  transfers between devices with their start and end apart: 2 -> 0, of which waited for: 1 -> 0; matrix products, arithmetic and copies ran while one was open for 21% -> 0% of each run, Pallas kernels for 0% -> 0%
where the time goes in v1:
time: 110 us; the launch traced here: 109 us
  Pallas kernels  103 us (94%)
  local copies, waits for them, and re-layouts  6.05 us (6%)
    pallas_call x1, Pallas kernels, outgoing_pool(): pl.pallas_call(out_kernel, out_shape=jax.ShapeDtypeStruct((GROUPS, NZ, 2,...  46.4 us
    pallas_call x1, Pallas kernels, translate(): pl.pallas_call(translate_kernel, out_shape=jax.ShapeDtypeStruct((128, 128...  42.5 us
    pallas_call x1, Pallas kernels, incoming_fields(): pl.pallas_call(in_kernel, out_shape=jax.ShapeDtypeStruct((256, 128), f32)...  14.3 us
    unnamed x29, local copies, waits for them, and re-layouts  5.94 us

profile of v1, /device:TPU:2, one launch (start us, length us, event | category | flops | bytes accessed | tf_op | source)
XLA Modules:
  0.0 109.3 jit_solution(5826546504478362410)
XLA Ops:
  0.0 0.0 copy-start
  0.0 0.0 copy-start.12
  0.0 0.9 copy-done
  0.9 0.1 reshape.22.rows_ref
  1.0 0.0 copy-done.12
  1.0 0.0 copy-start.4
  1.0 0.9 copy-done.4
  2.0 0.0 copy-start.5
  2.0 0.9 copy-done.5
  2.9 0.0 copy-start.7
  2.9 0.9 copy-done.7
  3.9 0.0 copy-start.8
  3.9 0.9 copy-done.8
  4.8 0.0 copy-start.1
  4.8 0.0 copy-start.9
  4.8 0.0 copy-start.10
  4.8 46.4 %outgoing.1 = f32[16,8,2,8,128]{4,3,2,1,0:T(8,128)S(1)} custom-call(f32[256,128]{1,0:T(8,128)S(1)} %bitcast.15, bf16[384,256]{1,0:T(8,128)(2,1)S(1)} %copy-done.7, bf16[64,96]{1,0:T(8,128)(2,1)S(1)} %copy-done.12, f32[8,64,128]{2,1,0:T(8,128)S(1)} %copy-done.5, f32[8,64,128]{2,1,0:T(8,128)S(1)} %copy-done.4), custom_call_target="tpu_custom_call" | custom-call | tf_op jit(solution)/shard_map/outgoing/pallas_call | solution.py:337
  51.2 0.0 copy-start.13
  51.2 0.0 copy-done.1
  51.2 0.0 copy-done.9
  51.2 0.0 copy-done.10
  51.2 0.6 copy-done.13
  51.8 0.0 copy-start.2
  51.8 0.0 copy-start.3
  51.8 0.0 copy-start.6
  51.8 0.0 copy-start.11
  51.8 42.5 %translate.1.field_ref = f32[128,128]{1,0:T(8,128)S(1)} custom-call(s32[64]{0:T(128)S(1)} %copy-done.13, s32[64,189]{1,0:T(8,128)S(1)} %copy-done.9, s32[64,189]{1,0:T(8,128)S(1)} %copy-done.10, s32[512]{0:T(512)S(1)} %reshape.22.rows_ref, f32[2048,128]{1,0:T(8,128)S(1)} %bitcast.12, f32[632,128]{1,0:T(8,128)S(1)} %bitcast.14), custom_call_target="tpu_custom_call" | custom-call | tf_op jit(solution)/shard_map/translate/pallas_call | solution.py:353
  94.3 0.0 copy-done.2
  94.3 0.0 copy-done.3
  94.3 0.0 copy-done.6
  94.3 0.0 copy-done.11
  94.3 14.3 %incoming.1 = f32[256,128]{1,0:T(8,128)S(1)} custom-call(f32[128,128]{1,0:T(8,128)S(1)} %translate.1.field_ref, bf16[768,128]{1,0:T(8,128)(2,1)S(1)} %copy-done.6, bf16[32,192]{1,0:T(8,128)(2,1)S(1)} %copy-done.11, f32[8,64,128]{2,1,0:T(8,128)S(1)} %copy-done.3, f32[8,64,128]{2,1,0:T(8,128)S(1)} %copy-done.2), custom_call_target="tpu_custom_call" | custom-call | tf_op jit(solution)/shard_map/incoming/pallas_call | solution.py:368
  108.6 0.7 copy.20
  (1 shorter events, 0.0 us)
Async XLA Ops:
  0.0 0.9 copy-start
  0.0 1.0 copy-start.12
  1.0 1.0 copy-start.4
  2.0 0.9 copy-start.5
  2.9 0.9 copy-start.7
  3.9 0.9 copy-start.8
  4.8 46.4 %copy-start.1 = (f32[316,2,128]{2,1,0:T(2,128)S(1)}, f32[316,2,128]{2,1,0:T(2,128)}, u32[]{:S(2)}) copy-start(f32[316,2,128]{2,1,0:T(2,128)} %param.15) | copy-start | bytes 970756
  4.8 46.4 %copy-start.9 = (s32[64,189]{1,0:T(8,128)S(1)}, s32[64,189]{1,0:T(8,128)}, u32[]{:S(2)}) copy-start(s32[64,189]{1,0:T(8,128)} %slot_hbm.1) | copy-start | bytes 145156
  4.8 46.4 %copy-start.10 = (s32[64,189]{1,0:T(8,128)S(1)}, s32[64,189]{1,0:T(8,128)}, u32[]{:S(2)}) copy-start(s32[64,189]{1,0:T(8,128)} %trans_hbm.1) | copy-start | bytes 145156
  51.2 0.7 copy-start.13
  51.8 42.5 %copy-start.2 = (f32[8,64,128]{2,1,0:T(8,128)S(1)}, f32[8,64,128]{2,1,0:T(8,128)}, u32[]{:S(2)}) copy-start(f32[8,64,128]{2,1,0:T(8,128)} %constant.35.clone.sin_ref) | copy-start | bytes 786436
  51.8 42.5 %copy-start.3 = (f32[8,64,128]{2,1,0:T(8,128)S(1)}, f32[8,64,128]{2,1,0:T(8,128)}, u32[]{:S(2)}) copy-start(f32[8,64,128]{2,1,0:T(8,128)} %constant.34.clone.cos_ref) | copy-start | bytes 786436
  51.8 42.5 %copy-start.6 = (bf16[768,128]{1,0:T(8,128)(2,1)S(1)}, bf16[768,128]{1,0:T(8,128)(2,1)}, u32[]{:S(2)}) copy-start(bf16[768,128]{1,0:T(8,128)(2,1)} %constant.32.clone.phi_ref) | copy-start | bytes 589828
  51.8 42.5 %copy-start.11 = (bf16[32,192]{1,0:T(8,128)(2,1)S(1)}, bf16[32,192]{1,0:T(8,128)(2,1)}, u32[]{:S(2)}) copy-start(bf16[32,192]{1,0:T(8,128)(2,1)} %constant.33.clone.theta_ref) | copy-start | bytes 36868

commit v2 on v0

v2 whole, which is shorter than its diff:
```python
import functools
import math

import jax
import jax.numpy as jnp
import numpy as np
from jax import lax
from jax.experimental import pallas as pl
from jax.experimental.pallas import tpu as pltpu
from jax.sharding import PartitionSpec as P

TC = 32
PC = 64
TP = 64
PP = 128
NTRANS = 316
NFAR = 189
CAP = 32
GROUPS = 16
SHIFT_PHASE = 2.7

NX = 8
NY = 8
NZ = 8
BF = jnp.bfloat16
MESH = pl.DeviceIdType.MESH


def interp_matrix(count_out, count_in, offset):
    target = (np.arange(count_out) + offset) / count_out
    source = (np.arange(count_in) + offset) / count_in
    spread = target[:, None] - source[None, :]
    orders = np.arange(1, count_in // 2)
    series = np.sum(np.cos(2.0 * math.pi * orders[None, None, :] * spread[:, :, None]), axis=2)
    return (1.0 + 2.0 * series + np.cos(math.pi * count_in * spread)) / count_in


def phase_tables():
    polar = math.pi * (np.arange(TP) + 0.5) / TP
    azimuth = 2.0 * math.pi * np.arange(PP) / PP
    wave_x = np.sin(polar)[:, None] * np.cos(azimuth)[None, :]
    wave_y = np.sin(polar)[:, None] * np.sin(azimuth)[None, :]
    wave_z = np.cos(polar)[:, None] * np.ones((1, PP))
    octant = np.arange(8)
    sign_x = (2 * (octant % 2) - 1)[:, None, None]
    sign_y = (2 * (octant // 2 % 2) - 1)[:, None, None]
    sign_z = (2 * (octant // 4) - 1)[:, None, None]
    angle = SHIFT_PHASE * (sign_x * wave_x + sign_y * wave_y + sign_z * wave_z)
    return np.cos(angle), np.sin(angle)


def halves(matrix):
    high = np.asarray(matrix, np.float32).astype(BF)
    low = (np.asarray(matrix, np.float32) - high.astype(np.float32)).astype(BF)
    return high, low


def constants():
    theta = interp_matrix(TP, TC, 0.5)
    phi = interp_matrix(PP, PC, 0.0)
    cosines, sines = phase_tables()
    pair = np.zeros((128, 256))
    pair[:64, :128] = phi.T
    pair[64:, 128:] = phi.T
    high, low = halves(pair)
    phi_out = np.concatenate([high, high, low], axis=0)
    theta_ba = np.concatenate([theta[:, 0::2], theta[:, 1::2]], axis=1)
    high, low = halves(theta_ba)
    theta_out = np.concatenate([high, high, low], axis=1)
    order = np.arange(64).reshape(8, 8).T.reshape(-1)
    high, low = halves(theta_ba.T[:, order])
    theta_in = np.concatenate([high, high, low], axis=1)
    back = np.zeros((256, 128))
    back[:128, :64] = phi
    back[128:, 64:] = phi
    high, low = halves(back * (TC * PC / (TP * PP)))
    phi_in = np.concatenate([high, high, low], axis=0)
    tables = np.concatenate([cosines[:4].reshape(256, 128), sines[:4].reshape(256, 128)]).astype(np.float32)
    return phi_out, theta_out, tables, theta_in, phi_in


def split(value):
    high = value.astype(BF)
    low = (value - high.astype(jnp.float32)).astype(BF)
    return high, low


def position():
    b = lax.axis_index("boxes")
    d = lax.axis_index("dirs")
    return b, b // 2, b % 2, d // NZ, d % NZ


def signal(barrier, device):
    pl.semaphore_signal(barrier, inc=1, device_id=device, device_id_type=MESH)


def one_hot(columns, first, tiles):
    lanes = lax.broadcasted_iota(jnp.int32, (16, 128), 1)
    numbers = [(lanes + (128 * k - first)).astype(jnp.float32).astype(BF) for k in range(tiles)]
    one, zero = jnp.ones((16, 128), BF), jnp.zeros((16, 128), BF)
    rows = []
    for e in range(0, 64, 2):
        column = jnp.concatenate([jnp.broadcast_to(columns[:, e + j:e + j + 1], (8, 128)) for j in range(2)], axis=0)
        column = column.astype(BF)
        rows.append([jnp.where(column == number, one, zero) for number in numbers])
    pieces = [jnp.concatenate([row[k] for row in rows], axis=0) for k in range(tiles)]
    return jnp.concatenate(pieces + pieces, axis=1)


def kernel(x_hbm, table_hbm, send_hbm, slot_hbm, trans_hbm, count_hbm, phi_out_hbm, theta_out_hbm, phases_hbm,
           theta_in_hbm, phi_in_hbm, out_ref,
           x_ref, table_ref, send_ref, slot_ref, trans_ref, count_ref, phi_out, theta_out, phases, theta_in, phi_in,
           wide_phi, send0, recv1, send2, pool, slot_at, trans_at, chosen, pick, sources, tables, gathered,
           back0, back1, back2, last, load_sem,
           ssem1, rsem1, ssem2, rsem2, ssem3, rsem3, ssem4, rsem4, ssem5, rsem5, ssem6, rsem6):
    f32 = jnp.float32
    b, x, core, y, z = position()
    d = y * NZ + z
    right = (x + 1) % NX * 2 + core
    left = (x + NX - 1) % NX * 2 + core
    other = x * 2 + 1 - core
    barrier = pltpu.get_barrier_semaphore()
    for k in range(1, NY):
        signal(barrier, (b, (y + k) % NY * NZ + z))
    for k in range(1, NZ):
        signal(barrier, (b, y * NZ + (z + k) % NZ))
    for device in (right, left, other):
        signal(barrier, (device, d))
    pairs = [(x_hbm, x_ref), (phi_out_hbm, phi_out), (theta_out_hbm, theta_out), (phases_hbm, phases),
             (table_hbm, table_ref.at[pl.ds(0, 2 * NTRANS)]), (trans_hbm, trans_ref), (count_hbm, count_ref),
             (slot_hbm, slot_ref), (send_hbm, send_ref), (theta_in_hbm, theta_in), (phi_in_hbm, phi_in)]
    loads = [pltpu.make_async_copy(src, dst, load_sem.at[i]) for i, (src, dst) in enumerate(pairs)]
    for load in loads:
        load.start()

    loads[0].wait()
    loads[1].wait()
    high, low = split(x_ref[...])
    both = jnp.dot(jnp.concatenate([high, low, high], axis=1), phi_out[...], preferred_element_type=f32)
    wide_phi[:256, :] = both[:, :128]
    wide_phi[256:, :] = both[:, 128:]
    loads[2].wait()
    loads[3].wait()
    real = jnp.zeros((TP, PP), f32)
    imag = jnp.zeros((TP, PP), f32)

    def child(o, r):
        return jnp.concatenate([wide_phi[pl.ds(half * 256 + o * 32 + r, 16, stride=2), :] for half in range(2)], axis=0)

    for o in range(4):
        near = [child(o, r) for r in range(2)]
        far = [child(7 - o, r) for r in range(2)]
        high, low = split(jnp.concatenate(
            [near[0] + far[0], near[1] + far[1], near[0] - far[0], near[1] - far[1]], axis=1))
        wide = jnp.dot(theta_out[...], jnp.concatenate([high, low, high], axis=0), preferred_element_type=f32)
        cosine, sine = phases[o * 64:o * 64 + 64, :], phases[256 + o * 64:256 + o * 64 + 64, :]
        real += cosine * wide[:, :128] - sine * wide[:, 384:]
        imag += sine * wide[:, 256:384] + cosine * wide[:, 128:256]
    for i in range(NY):
        send0[i * 16:i * 16 + 8, :] = real[i * 8:i * 8 + 8]
        send0[i * 16 + 8:i * 16 + 16, :] = imag[i * 8:i * 8 + 8]

    pl.semaphore_wait(barrier, NY + NZ - 2 + 3)

    def along_y(source, landing, ssem, rsem, k, peer_slot):
        target = (y + k) % NY
        return pltpu.make_async_remote_copy(
            src_ref=source.at[pl.ds(pl.multiple_of(target * 16, 16), 16)],
            dst_ref=landing.at[pl.ds(pl.multiple_of(peer_slot * 16, 16), 16)],
            send_sem=ssem.at[k], recv_sem=rsem.at[k],
            device_id=(b, target * NZ + z), device_id_type=MESH)

    def along_z(source, landing, ssem, rsem, k, peer_slot):
        target = (z + k) % NZ
        return pltpu.make_async_remote_copy(
            src_ref=source.at[target], dst_ref=landing.at[peer_slot],
            send_sem=ssem.at[k], recv_sem=rsem.at[k],
            device_id=(b, y * NZ + target), device_id_type=MESH)

    far_first = (4, 3, 5, 2, 6, 1, 7)
    for k in far_first:
        along_y(send0, recv1, ssem1, rsem1, k, y).start()
    mine = pl.ds(pl.multiple_of(y * 16, 16), 16)
    recv1[mine, :] = send0[mine, :]

    table_ref[2 * NTRANS:, :] = jnp.zeros((768 - 2 * NTRANS, 128), f32)
    for i in range(4, 7):
        loads[i].wait()
    for r in range(2):
        high, low = split(table_ref[pl.ds(r, 384, stride=2), :])
        tables[:384, r * 128:(r + 1) * 128] = high
        tables[384:, r * 128:(r + 1) * 128] = low
    diagonal = lax.broadcasted_iota(jnp.int32, (64, 64), 0) == lax.broadcasted_iota(jnp.int32, (64, 64), 1)
    count = jnp.broadcast_to(count_ref[...].astype(f32), (64, 64))
    count = jnp.sum(jnp.where(diagonal, count, 0.0), axis=1, keepdims=True)
    entry = lax.broadcasted_iota(jnp.int32, (64, NFAR), 1).astype(f32)
    trans_at[...] = jnp.full((64, 256), -256.0, f32)
    trans_at[:, :NFAR] = jnp.where(entry < count, (trans_ref[...] - 158).astype(f32), -256.0)

    def gather_tables(i, carry):
        columns = trans_at[pl.ds(pl.multiple_of(i * 8, 8), 8), :]
        for chunk in range(3):
            rows = pl.ds(pl.multiple_of((i * 3 + chunk) * 512, 512), 512)
            gathered[rows, :] = jnp.dot(one_hot(columns[:, chunk * 64:chunk * 64 + 64], 158, 3), tables[...],
                                        preferred_element_type=f32)
        return carry

    lax.fori_loop(0, 3, gather_tables, 0)
    for k in range(1, NY):
        along_y(send0, recv1, ssem1, rsem1, k, (y + NY - k) % NY).wait_recv()
    for target in range(NZ):
        for r in range(2):
            send2[target, r] = recv1[pl.ds(r * 8 + target, 8, stride=16), :]
    for k in far_first:
        along_z(send2, pool.at[b], ssem2, rsem2, k, z).start()
    pool[b, z] = send2[z]

    loads[7].wait()
    loads[8].wait()
    slot_at[...] = jnp.zeros((64, 256), f32)
    slot_at[:, :NFAR] = (slot_ref[...] - 256).astype(f32)
    chosen[...] = jnp.zeros((16, 128), f32)
    for g in range(GROUPS):
        chosen[g:g + 1, :CAP] = send_ref[g, pl.ds(b, 1), :].astype(f32)
    across_rows = chosen[...].T
    place = lax.broadcasted_iota(jnp.int32, (CAP, 64), 1)
    place = (place % 8 * 8 + place // 8).astype(f32)
    for g in range(GROUPS):
        pick[g * CAP:(g + 1) * CAP, :64] = jnp.where(
            jnp.broadcast_to(across_rows[:CAP, g:g + 1], (CAP, 64)) == place, 1.0, 0.0).astype(BF)
    lax.fori_loop(3, 6, gather_tables, 0)
    for k in range(1, NZ):
        along_z(send2, pool.at[b], ssem2, rsem2, k, (z + NZ - k) % NZ).wait_recv()

    def compact(g):
        block = pool[g]
        parts = [split(block[:, r].reshape(64, 128)) for r in range(2)]
        rows = pl.ds(pl.multiple_of(g * CAP, CAP), CAP)
        sent = jnp.dot(pick[rows, :64], jnp.concatenate([parts[0][0], parts[1][0], parts[0][1], parts[1][1]], axis=1),
                       preferred_element_type=f32).astype(BF)
        sources[rows, :] = sent[:, :256]
        sources[pl.ds(pl.multiple_of(512 + g * CAP, CAP), CAP), :] = sent[:, 256:]

    slots = [(s, h) for s in range(3) for h in range(2)] + [(3, 0)]

    def from_origin(way, back):
        return (x + NX - back) % NX if way == 0 else (x + back) % NX

    def ring(way, n, sent):
        s, h = slots[n]
        h = way if s == 3 else h
        block = pool.at[from_origin(way, s if sent else s + 1) * 2 + core, pl.ds(h * 4, 4)]
        return pltpu.make_async_remote_copy(
            src_ref=block, dst_ref=block, send_sem=ssem3.at[way, n], recv_sem=rsem3.at[way, n],
            device_id=((right, left)[way], d), device_id_type=MESH)

    def across(n, mine):
        if n == 0:
            back, way, part = 0, 0, pl.ds(0, 8)
        else:
            back, way = (n + 1) // 2, (n + 1) % 2
            part = pl.ds(0, 8) if back < 4 else pl.ds(way * 4, 4)
        block = pool.at[from_origin(way, back) * 2 + (core if mine else 1 - core), part]
        return pltpu.make_async_remote_copy(
            src_ref=block, dst_ref=block, send_sem=ssem4.at[n], recv_sem=rsem4.at[n],
            device_id=(other, d), device_id_type=MESH)

    for n in range(2):
        ring(0, n, True).start()
        ring(1, n, True).start()
    across(0, True).start()
    compact(b)
    lax.fori_loop(6, 8, gather_tables, 0)
    for s in range(4):
        for n, (step, h) in enumerate(slots):
            if step != s:
                continue
            for way in range(2):
                ring(way, n, False).wait_recv()
                if s < 2 or (s == 2 and h == way):
                    ring(way, n + 2 if s < 2 else 6, True).start()
        for way in range(2):
            across(2 * s + 1 + way, True).start()
        for way in range(2 if s < 3 else 1):
            compact(from_origin(way, s + 1) * 2 + core)
        for n in ((0,), (1, 2), (3, 4), (5, 6))[s]:
            across(n, False).wait_recv()
            way, back = (0, 0) if n == 0 else ((n + 1) % 2, (n + 1) // 2)
            compact(from_origin(way, back) * 2 + 1 - core)
    across(7, False).wait_recv()
    across(8, False).wait_recv()
    compact(from_origin(0, 4) * 2 + 1 - core)

    def one_owner(i, carry):
        k = 4 + (i + 1) // 2 * (1 - 2 * (i % 2))
        target = (y + k) % NY
        columns = slot_at[pl.ds(pl.multiple_of(target * 8, 8), 8), :]
        real = jnp.zeros((8, 128), f32)
        imag = jnp.zeros((8, 128), f32)
        for chunk in range(3):
            field = jnp.dot(one_hot(columns[:, chunk * 64:chunk * 64 + 64], 256, 4), sources[...],
                            preferred_element_type=f32)
            weight = gathered[pl.ds(pl.multiple_of((target * 3 + chunk) * 512, 512), 512), :]
            fr, fi, wr, wi = field[:, :128], field[:, 128:], weight[:, :128], weight[:, 128:]
            real += jnp.sum((fr * wr - fi * wi).reshape(64, 8, 128), axis=0)
            imag += jnp.sum((fr * wi + fi * wr).reshape(64, 8, 128), axis=0)
        back0[pl.ds(pl.multiple_of(target * 16, 16), 8), :] = real
        back0[pl.ds(pl.multiple_of(target * 16 + 8, 8), 8), :] = imag

        @pl.when(i < 7)
        def _():
            along_y(back0, back1, ssem5, rsem5, k, y).start()
        return carry

    lax.fori_loop(0, NY, one_owner, 0)
    back1[mine, :] = back0[mine, :]
    for load in loads[9:]:
        load.wait()
    for k in range(1, NY):
        along_y(back0, back1, ssem5, rsem5, k, (y + NY - k) % NY).wait_recv()
    for target in range(NZ):
        for r in range(2):
            back2[target, r] = back1[pl.ds(r * 8 + target, 8, stride=16), :]
    for k in far_first:
        along_z(back2, last, ssem6, rsem6, k, z).start()
    last[z] = back2[z]
    for k in range(1, NY):
        along_y(send0, recv1, ssem1, rsem1, k, y).wait_send()
        along_z(send2, pool.at[b], ssem2, rsem2, k, z).wait_send()
        along_y(back0, back1, ssem5, rsem5, k, y).wait_send()
    for n in range(7):
        for way in range(2):
            ring(way, n, True).wait_send()
    for n in range(9):
        across(n, True).wait_send()
    for k in range(1, NZ):
        along_z(back2, last, ssem6, rsem6, k, (z + NZ - k) % NZ).wait_recv()

    real = last[:, 0].reshape(TP, PP)
    imag = last[:, 1].reshape(TP, PP)
    narrow = [None] * 16
    for o in range(4):
        cosine, sine = [jnp.concatenate([phases[pl.ds(half * 256 + o * 64 + i, 8, stride=8), :] for i in range(NZ)], axis=0)
                        for half in range(2)]
        high, low = split(jnp.concatenate([cosine * real, sine * imag, cosine * imag, sine * real], axis=1))
        rows = jnp.dot(theta_in[...], jnp.concatenate([high, low, high], axis=0), preferred_element_type=f32)
        cr, si, ci, sr = [rows[:, i * 128:(i + 1) * 128] for i in range(4)]
        for n, value in ((o, cr + si), (7 - o, cr - si)):
            narrow[n * 2] = jnp.concatenate([value[:16], value[16:]], axis=1)
        for n, value in ((o, ci - sr), (7 - o, ci + sr)):
            narrow[n * 2 + 1] = jnp.concatenate([value[:16], value[16:]], axis=1)
    high, low = split(jnp.concatenate(narrow, axis=0))
    result = jnp.dot(jnp.concatenate([high, low, high], axis=1), phi_in[...], preferred_element_type=f32)
    for o in range(8):
        for r in range(2):
            n = o * 2 + r
            out_ref[pl.ds(o * 32 + r, 16, stride=2), :] = result[n * 16:(n + 1) * 16]
    for k in range(1, NZ):
        along_z(back2, last, ssem6, rsem6, k, z).wait_send()


def whole():
    return pl.BlockSpec(memory_space=pltpu.VMEM)


def dma(*shape):
    return pltpu.SemaphoreType.DMA(shape)


def whole_step(fields, table, send_rows, slots, trans, counts, const):
    f32, i32 = jnp.float32, jnp.int32
    vmem = pltpu.VMEM
    tile = (NZ, 2, NY, 128)
    return pl.pallas_call(
        kernel,
        out_shape=jax.ShapeDtypeStruct((256, 128), f32),
        in_specs=[pl.BlockSpec(memory_space=pl.ANY)] * 11, out_specs=whole(),
        scratch_shapes=[
            vmem((256, 128), f32), vmem((768, 128), f32), vmem((GROUPS, GROUPS, CAP), i32), vmem((64, NFAR), i32),
            vmem((64, NFAR), i32), vmem((1, 64), i32), vmem((384, 256), BF), vmem((64, 96), BF), vmem((512, 128), f32),
            vmem((32, 192), BF), vmem((768, 128), BF),
            vmem((512, 128), f32), vmem((128, 128), f32), vmem((128, 128), f32), vmem(tile, f32),
            vmem((GROUPS,) + tile, f32), vmem((64, 256), f32), vmem((64, 256), f32), vmem((16, 128), f32),
            vmem((GROUPS * CAP, 128), BF), vmem((2 * GROUPS * CAP, 256), BF), vmem((768, 256), BF),
            vmem((24 * 512, 256), f32),
            vmem((128, 128), f32), vmem((128, 128), f32), vmem(tile, f32), vmem(tile, f32), dma(11),
            dma(8), dma(8), dma(8), dma(8), dma(2, 7), dma(2, 7), dma(9), dma(9), dma(8), dma(8), dma(8), dma(8)],
        compiler_params=pltpu.CompilerParams(collective_id=0, has_side_effects=True, vmem_limit_bytes=60 << 20),
        name="level_pair",
    )(fields, table, send_rows, slots, trans, counts, *const)


def on_device(const, child_outgoing, trans_table, send_rows, far_slot, far_trans, far_count):
    fields = child_outgoing.reshape(8, 2, 16, 128).transpose(0, 2, 1, 3).reshape(256, 128)
    out = whole_step(fields, trans_table.reshape(NTRANS * 2, 128), send_rows, far_slot, far_trans,
                     far_count.reshape(1, 64), const)
    return out.reshape(8, 16, 2, 128).transpose(0, 2, 1, 3).reshape(8, 2, 2048)


def solution(mesh):
    placed = (
        P(("boxes", "dirs"), None, None),
        P(None, None, "dirs"),
        P(),
        P("boxes", None),
        P("boxes", None),
        P("boxes"),
    )
    const = constants()
    return jax.shard_map(
        functools.partial(on_device, const),
        mesh=mesh,
        in_specs=placed,
        out_specs=P(("boxes", "dirs"), None, None),
        check_vma=False,
    )
```

time: 356 us -> 64 us (0.18)
  the two profiles are of different devices: /device:TPU:2 before, /device:TPU:1 now
where the time goes in v2:
time: 64 us; the launch traced here: 63.9 us
  Pallas kernels  62.3 us (97%)
  local copies, waits for them, and re-layouts  1.57 us (2%)
    pallas_call x1, Pallas kernels, whole_step(): pl.pallas_call(kernel, out_shape=jax.ShapeDtypeStruct((256, 128), f32), i...  62.3 us
    unnamed x1, local copies, waits for them, and re-layouts  1.57 us

profile of v2, /device:TPU:1, one launch (start us, length us, event | category | flops | bytes accessed | tf_op | source)
XLA Modules:
  0.0 63.9 jit_solution(10411652990097133557)
XLA Ops:
  0.0 62.3 %level_pair.1 = f32[256,128]{1,0:T(8,128)} custom-call(f32[256,128]{1,0:T(8,128)} %bitcast.14, f32[632,128]{1,0:T(8,128)} %bitcast.13, s32[16,16,32]{2,1,0:T(8,128)} %send_hbm.1, s32[64,189]{1,0:T(8,128)} %slot_hbm.1, s32[64,189]{1,0:T(8,128)} %trans_hbm.1, s32[1,64]{1,0:T(1,128)} %bitcast.15, bf16[384,256]{1,0:T(8,128)(2,1)} %constant.10.clone.phi_out_hbm, ...), custom_call_target="tpu_custom_call" | custom-call | tf_op jit(solution)/shard_map/level_pair/pallas_call | solution.py:375
  62.3 1.6 %copy.15 = f32[8,2,2048]{2,1,0:T(2,128)} copy(f32[8,2,2048]{2,1,0:T(2,128)} %bitcast.12) | data formatting | bytes 262144

commit v3 on v2

--- a/solution.py
+++ b/solution.py
@@ -24,6 +24,7 @@
 NZ = 8
 BF = jnp.bfloat16
 MESH = pl.DeviceIdType.MESH
+NEAR = (0, 1, 7, 2, 6, 3, 5, 4)
 
 
 def interp_matrix(count_out, count_in, offset):
@@ -108,11 +109,18 @@
     return jnp.concatenate(pieces + pieces, axis=1)
 
 
+def by_chunk(ref, lists, fill):
+    for chunk in range(3):
+        width = min(64, NFAR - chunk * 64)
+        ref[chunk * 64:chunk * 64 + 64, :] = jnp.full((64, 128), fill, jnp.float32)
+        ref[chunk * 64:chunk * 64 + 64, :width] = lists[:, chunk * 64:chunk * 64 + width]
+
+
 def kernel(x_hbm, table_hbm, send_hbm, slot_hbm, trans_hbm, count_hbm, phi_out_hbm, theta_out_hbm, phases_hbm,
            theta_in_hbm, phi_in_hbm, out_ref,
            x_ref, table_ref, send_ref, slot_ref, trans_ref, count_ref, phi_out, theta_out, phases, theta_in, phi_in,
            wide_phi, send0, recv1, send2, pool, slot_at, trans_at, chosen, pick, sources, tables, gathered,
-           back0, back1, back2, last, load_sem,
+           halfway, back0, back1, back2, last, load_sem,
            ssem1, rsem1, ssem2, rsem2, ssem3, rsem3, ssem4, rsem4, ssem5, rsem5, ssem6, rsem6):
     f32 = jnp.float32
     b, x, core, y, z = position()
@@ -121,9 +129,9 @@
     left = (x + NX - 1) % NX * 2 + core
     other = x * 2 + 1 - core
     barrier = pltpu.get_barrier_semaphore()
-    for k in range(1, NY):
+    far_first = (4, 3, 5, 2, 6, 1, 7)
+    for k in far_first:
         signal(barrier, (b, (y + k) % NY * NZ + z))
-    for k in range(1, NZ):
         signal(barrier, (b, y * NZ + (z + k) % NZ))
     for device in (right, left, other):
         signal(barrier, (device, d))
@@ -174,11 +182,10 @@
     def along_z(source, landing, ssem, rsem, k, peer_slot):
         target = (z + k) % NZ
         return pltpu.make_async_remote_copy(
-            src_ref=source.at[target], dst_ref=landing.at[peer_slot],
+            src_ref=source.at[target], dst_ref=landing.at[peer_slot if peer_slot is not None else NEAR.index(-k % NZ)],
             send_sem=ssem.at[k], recv_sem=rsem.at[k],
             device_id=(b, y * NZ + target), device_id_type=MESH)
 
-    far_first = (4, 3, 5, 2, 6, 1, 7)
     for k in far_first:
         along_y(send0, recv1, ssem1, rsem1, k, y).start()
     mine = pl.ds(pl.multiple_of(y * 16, 16), 16)
@@ -195,57 +202,59 @@
     count = jnp.broadcast_to(count_ref[...].astype(f32), (64, 64))
     count = jnp.sum(jnp.where(diagonal, count, 0.0), axis=1, keepdims=True)
     entry = lax.broadcasted_iota(jnp.int32, (64, NFAR), 1).astype(f32)
-    trans_at[...] = jnp.full((64, 256), -256.0, f32)
-    trans_at[:, :NFAR] = jnp.where(entry < count, (trans_ref[...] - 158).astype(f32), -256.0)
-
-    def gather_tables(i, carry):
-        columns = trans_at[pl.ds(pl.multiple_of(i * 8, 8), 8), :]
-        for chunk in range(3):
-            rows = pl.ds(pl.multiple_of((i * 3 + chunk) * 512, 512), 512)
-            gathered[rows, :] = jnp.dot(one_hot(columns[:, chunk * 64:chunk * 64 + 64], 158, 3), tables[...],
-                                        preferred_element_type=f32)
-        return carry
-
-    lax.fori_loop(0, 3, gather_tables, 0)
+    by_chunk(trans_at, jnp.where(entry < count, (trans_ref[...] - 158).astype(f32), -256.0), -256.0)
+
+    def gather_tables(first, until):
+        def one(i, carry):
+            columns = trans_at[pl.ds(pl.multiple_of(i * 8, 8), 8), :]
+            gathered[pl.ds(pl.multiple_of(i * 512, 512), 512), :] = jnp.dot(
+                one_hot(columns[:, :64], 158, 3), tables[...], preferred_element_type=f32)
+            return carry
+        lax.fori_loop(first, until, one, 0)
+
+    gather_tables(0, 9)
     for k in range(1, NY):
         along_y(send0, recv1, ssem1, rsem1, k, (y + NY - k) % NY).wait_recv()
     for target in range(NZ):
         for r in range(2):
             send2[target, r] = recv1[pl.ds(r * 8 + target, 8, stride=16), :]
     for k in far_first:
-        along_z(send2, pool.at[b], ssem2, rsem2, k, z).start()
-    pool[b, z] = send2[z]
+        along_z(send2, pool.at[b], ssem2, rsem2, k, None).start()
+    pool[b, 0] = send2[z]
 
     loads[7].wait()
     loads[8].wait()
-    slot_at[...] = jnp.zeros((64, 256), f32)
-    slot_at[:, :NFAR] = (slot_ref[...] - 256).astype(f32)
+    slot = slot_ref[...]
+    chip = ((slot >> 6) - x) & 7
+    chip = jnp.where(chip < 4, 2 * chip, 15 - 2 * chip)
+    by_chunk(slot_at, (chip * 64 + (slot & 63) - 256).astype(f32), 0.0)
     chosen[...] = jnp.zeros((16, 128), f32)
     for g in range(GROUPS):
         chosen[g:g + 1, :CAP] = send_ref[g, pl.ds(b, 1), :].astype(f32)
     across_rows = chosen[...].T
     place = lax.broadcasted_iota(jnp.int32, (CAP, 64), 1)
-    place = (place % 8 * 8 + place // 8).astype(f32)
+    near = place >> 3
+    near = jnp.where((near & 1) == 1, (near + 1) >> 1, 8 - (near >> 1))
+    place = ((place & 7) * 8 + ((near + z) & 7)).astype(f32)
     for g in range(GROUPS):
         pick[g * CAP:(g + 1) * CAP, :64] = jnp.where(
             jnp.broadcast_to(across_rows[:CAP, g:g + 1], (CAP, 64)) == place, 1.0, 0.0).astype(BF)
-    lax.fori_loop(3, 6, gather_tables, 0)
-    for k in range(1, NZ):
-        along_z(send2, pool.at[b], ssem2, rsem2, k, (z + NZ - k) % NZ).wait_recv()
-
-    def compact(g):
-        block = pool[g]
+    def from_origin(way, back):
+        return (x + NX - back) % NX if way == 0 else (x + back) % NX
+
+    def compact(way, back, parity):
+        block = pool[from_origin(way, back) * 2 + parity]
+        rank = 7 if back == 4 else 0 if back == 0 else 2 * back - 1 + way
+        g = from_origin(way, back) * 2 + parity
         parts = [split(block[:, r].reshape(64, 128)) for r in range(2)]
         rows = pl.ds(pl.multiple_of(g * CAP, CAP), CAP)
         sent = jnp.dot(pick[rows, :64], jnp.concatenate([parts[0][0], parts[1][0], parts[0][1], parts[1][1]], axis=1),
                        preferred_element_type=f32).astype(BF)
-        sources[rows, :] = sent[:, :256]
-        sources[pl.ds(pl.multiple_of(512 + g * CAP, CAP), CAP), :] = sent[:, 256:]
+        first = pl.multiple_of(rank // 4 * 512 + rank % 4 * 64 + parity * CAP, CAP)
+        sources[pl.ds(first, CAP), :] = sent[:, :256]
+        sources[pl.ds(pl.multiple_of(first + 256, CAP), CAP), :] = sent[:, 256:]
 
     slots = [(s, h) for s in range(3) for h in range(2)] + [(3, 0)]
-
-    def from_origin(way, back):
-        return (x + NX - back) % NX if way == 0 else (x + back) % NX
 
     def ring(way, n, sent):
         s, h = slots[n]
@@ -266,45 +275,72 @@
             src_ref=block, dst_ref=block, send_sem=ssem4.at[n], recv_sem=rsem4.at[n],
             device_id=(other, d), device_id_type=MESH)
 
-    for n in range(2):
-        ring(0, n, True).start()
-        ring(1, n, True).start()
+    def products(target, late):
+        pieces = [one_hot(slot_at[pl.ds(pl.multiple_of(chunk * 64 + target * 8, 8), 8), :][:, :64], 0 if late else 256, 2)
+                  for chunk in range(3)]
+        field = jnp.dot(jnp.concatenate(pieces, axis=0), sources[late * 512:late * 512 + 512, :],
+                        preferred_element_type=f32)
+        real = jnp.zeros((8, 128), f32)
+        imag = jnp.zeros((8, 128), f32)
+        for chunk in range(3):
+            weight = gathered[pl.ds(pl.multiple_of((chunk * 8 + target) * 512, 512), 512), :]
+            rows = field[chunk * 512:chunk * 512 + 512]
+            fr, fi, wr, wi = rows[:, :128], rows[:, 128:], weight[:, :128], weight[:, 128:]
+            real += jnp.sum((fr * wr - fi * wi).reshape(64, 8, 128), axis=0)
+            imag += jnp.sum((fr * wi + fi * wr).reshape(64, 8, 128), axis=0)
+        return real, imag
+
+    def early(first, until):
+        def one(i, carry):
+            real, imag = products(i, 0)
+            halfway[pl.ds(pl.multiple_of(i * 16, 16), 8), :] = real
+            halfway[pl.ds(pl.multiple_of(i * 16 + 8, 8), 8), :] = imag
+            return carry
+        lax.fori_loop(first, until, one, 0)
+
+    gather_tables(9, 13)
+    for half in range(2):
+        for k in range(1, NZ):
+            if NEAR.index(-k % NZ) // 4 == half:
+                along_z(send2, pool.at[b], ssem2, rsem2, k, None).wait_recv()
+        for way in range(2):
+            ring(way, half, True).start()
+        if half == 0:
+            gather_tables(13, 16)
     across(0, True).start()
-    compact(b)
-    lax.fori_loop(6, 8, gather_tables, 0)
-    for s in range(4):
-        for n, (step, h) in enumerate(slots):
-            if step != s:
-                continue
-            for way in range(2):
-                ring(way, n, False).wait_recv()
-                if s < 2 or (s == 2 and h == way):
-                    ring(way, n + 2 if s < 2 else 6, True).start()
+    compact(0, 0, core)
+    unit = 16
+    for n, (s, h) in enumerate(slots):
+        for way in range(2):
+            ring(way, n, False).wait_recv()
+            if s < 2 or (s == 2 and h == way):
+                ring(way, n + 2 if s < 2 else 6, True).start()
+        if unit < 24:
+            gather_tables(unit, unit + 2)
+            unit += 2
+        if h == 0 and s < 3:
+            continue
         for way in range(2):
             across(2 * s + 1 + way, True).start()
         for way in range(2 if s < 3 else 1):
-            compact(from_origin(way, s + 1) * 2 + core)
-        for n in ((0,), (1, 2), (3, 4), (5, 6))[s]:
-            across(n, False).wait_recv()
-            way, back = (0, 0) if n == 0 else ((n + 1) % 2, (n + 1) // 2)
-            compact(from_origin(way, back) * 2 + 1 - core)
+            compact(way, s + 1, core)
+        for m in ((0,), (1, 2), (3, 4), (5, 6))[s]:
+            across(m, False).wait_recv()
+            way, back = (0, 0) if m == 0 else ((m + 1) % 2, (m + 1) // 2)
+            compact(way, back, 1 - core)
+        if s == 2:
+            early(0, 5)
+    early(5, 8)
     across(7, False).wait_recv()
     across(8, False).wait_recv()
-    compact(from_origin(0, 4) * 2 + 1 - core)
+    compact(0, 4, 1 - core)
 
     def one_owner(i, carry):
         k = 4 + (i + 1) // 2 * (1 - 2 * (i % 2))
         target = (y + k) % NY
-        columns = slot_at[pl.ds(pl.multiple_of(target * 8, 8), 8), :]
-        real = jnp.zeros((8, 128), f32)
-        imag = jnp.zeros((8, 128), f32)
-        for chunk in range(3):
-            field = jnp.dot(one_hot(columns[:, chunk * 64:chunk * 64 + 64], 256, 4), sources[...],
-                            preferred_element_type=f32)
-            weight = gathered[pl.ds(pl.multiple_of((target * 3 + chunk) * 512, 512), 512), :]
-            fr, fi, wr, wi = field[:, :128], field[:, 128:], weight[:, :128], weight[:, 128:]
-            real += jnp.sum((fr * wr - fi * wi).reshape(64, 8, 128), axis=0)
-            imag += jnp.sum((fr * wi + fi * wr).reshape(64, 8, 128), axis=0)
+        real, imag = products(target, 1)
+        real += halfway[pl.ds(pl.multiple_of(target * 16, 16), 8), :]
+        imag += halfway[pl.ds(pl.multiple_of(target * 16 + 8, 8), 8), :]
         back0[pl.ds(pl.multiple_of(target * 16, 16), 8), :] = real
         back0[pl.ds(pl.multiple_of(target * 16 + 8, 8), 8), :] = imag
 
@@ -327,7 +363,7 @@
     last[z] = back2[z]
     for k in range(1, NY):
         along_y(send0, recv1, ssem1, rsem1, k, y).wait_send()
-        along_z(send2, pool.at[b], ssem2, rsem2, k, z).wait_send()
+        along_z(send2, pool.at[b], ssem2, rsem2, k, None).wait_send()
         along_y(back0, back1, ssem5, rsem5, k, y).wait_send()
     for n in range(7):
         for way in range(2):
@@ -381,10 +417,10 @@
             vmem((64, NFAR), i32), vmem((1, 64), i32), vmem((384, 256), BF), vmem((64, 96), BF), vmem((512, 128), f32),
             vmem((32, 192), BF), vmem((768, 128), BF),
             vmem((512, 128), f32), vmem((128, 128), f32), vmem((128, 128), f32), vmem(tile, f32),
-            vmem((GROUPS,) + tile, f32), vmem((64, 256), f32), vmem((64, 256), f32), vmem((16, 128), f32),
+            vmem((GROUPS,) + tile, f32), vmem((192, 128), f32), vmem((192, 128), f32), vmem((16, 128), f32),
             vmem((GROUPS * CAP, 128), BF), vmem((2 * GROUPS * CAP, 256), BF), vmem((768, 256), BF),
             vmem((24 * 512, 256), f32),
-            vmem((128, 128), f32), vmem((128, 128), f32), vmem(tile, f32), vmem(tile, f32), dma(11),
+            vmem((128, 128), f32), vmem((128, 128), f32), vmem((128, 128), f32), vmem(tile, f32), vmem(tile, f32), dma(11),
             dma(8), dma(8), dma(8), dma(8), dma(2, 7), dma(2, 7), dma(9), dma(9), dma(8), dma(8), dma(8), dma(8)],
         compiler_params=pltpu.CompilerParams(collective_id=0, has_side_effects=True, vmem_limit_bytes=60 << 20),
         name="level_pair",

time: 64 us -> 63.6 us (level)
  the two profiles are of different devices: /device:TPU:1 before, /device:TPU:6 now
where the time goes in v3:
time: 63.6 us; the launch traced here: 63.4 us
  Pallas kernels  61.8 us (97%)
  local copies, waits for them, and re-layouts  1.57 us (2%)
    pallas_call x1, Pallas kernels, whole_step(): pl.pallas_call(kernel, out_shape=jax.ShapeDtypeStruct((256, 128), f32), i...  61.8 us
    unnamed x1, local copies, waits for them, and re-layouts  1.57 us

profile of v3, /device:TPU:6, one launch (start us, length us, event | category | flops | bytes accessed | tf_op | source)
XLA Modules:
  0.0 63.4 jit_solution(5684638406181426238)
XLA Ops:
  0.0 61.8 %level_pair.1 = f32[256,128]{1,0:T(8,128)} custom-call(f32[256,128]{1,0:T(8,128)} %bitcast.14, f32[632,128]{1,0:T(8,128)} %bitcast.13, s32[16,16,32]{2,1,0:T(8,128)} %send_hbm.1, s32[64,189]{1,0:T(8,128)} %slot_hbm.1, s32[64,189]{1,0:T(8,128)} %trans_hbm.1, s32[1,64]{1,0:T(1,128)} %bitcast.15, bf16[384,256]{1,0:T(8,128)(2,1)} %constant.10.clone.phi_out_hbm, ...), custom_call_target="tpu_custom_call" | custom-call | tf_op jit(solution)/shard_map/level_pair/pallas_call | solution.py:411
  61.8 1.6 %copy.15 = f32[8,2,2048]{2,1,0:T(2,128)} copy(f32[8,2,2048]{2,1,0:T(2,128)} %bitcast.12) | data formatting | bytes 262144

commit v4 on v3

--- a/solution.py
+++ b/solution.py
@@ -107,6 +107,10 @@
         rows.append([jnp.where(column == number, one, zero) for number in numbers])
     pieces = [jnp.concatenate([row[k] for row in rows], axis=0) for k in range(tiles)]
     return jnp.concatenate(pieces + pieces, axis=1)
+
+
+def take(ref, sem):
+    pltpu.make_async_copy(ref, ref, sem).wait()
 
 
 def by_chunk(ref, lists, fill):
@@ -176,14 +180,14 @@
         return pltpu.make_async_remote_copy(
             src_ref=source.at[pl.ds(pl.multiple_of(target * 16, 16), 16)],
             dst_ref=landing.at[pl.ds(pl.multiple_of(peer_slot * 16, 16), 16)],
-            send_sem=ssem.at[k], recv_sem=rsem.at[k],
+            send_sem=ssem, recv_sem=rsem,
             device_id=(b, target * NZ + z), device_id_type=MESH)
 
     def along_z(source, landing, ssem, rsem, k, peer_slot):
         target = (z + k) % NZ
         return pltpu.make_async_remote_copy(
             src_ref=source.at[target], dst_ref=landing.at[peer_slot if peer_slot is not None else NEAR.index(-k % NZ)],
-            send_sem=ssem.at[k], recv_sem=rsem.at[k],
+            send_sem=ssem, recv_sem=rsem,
             device_id=(b, y * NZ + target), device_id_type=MESH)
 
     for k in far_first:
@@ -213,8 +217,7 @@
         lax.fori_loop(first, until, one, 0)
 
     gather_tables(0, 9)
-    for k in range(1, NY):
-        along_y(send0, recv1, ssem1, rsem1, k, (y + NY - k) % NY).wait_recv()
+    take(recv1.at[pl.ds(0, 112)], rsem1)
     for target in range(NZ):
         for r in range(2):
             send2[target, r] = recv1[pl.ds(r * 8 + target, 8, stride=16), :]
@@ -254,25 +257,18 @@
         sources[pl.ds(first, CAP), :] = sent[:, :256]
         sources[pl.ds(pl.multiple_of(first + 256, CAP), CAP), :] = sent[:, 256:]
 
-    slots = [(s, h) for s in range(3) for h in range(2)] + [(3, 0)]
-
-    def ring(way, n, sent):
-        s, h = slots[n]
-        h = way if s == 3 else h
-        block = pool.at[from_origin(way, s if sent else s + 1) * 2 + core, pl.ds(h * 4, 4)]
+    def ring(way, s):
+        block = pool.at[from_origin(way, s) * 2 + core]
+        if s == 3:
+            block = block.at[pl.ds(way * 4, 4)]
         return pltpu.make_async_remote_copy(
-            src_ref=block, dst_ref=block, send_sem=ssem3.at[way, n], recv_sem=rsem3.at[way, n],
+            src_ref=block, dst_ref=block, send_sem=ssem3, recv_sem=rsem3.at[s],
             device_id=((right, left)[way], d), device_id_type=MESH)
 
-    def across(n, mine):
-        if n == 0:
-            back, way, part = 0, 0, pl.ds(0, 8)
-        else:
-            back, way = (n + 1) // 2, (n + 1) % 2
-            part = pl.ds(0, 8) if back < 4 else pl.ds(way * 4, 4)
-        block = pool.at[from_origin(way, back) * 2 + (core if mine else 1 - core), part]
+    def across(way, back):
+        block = pool.at[from_origin(way, back) * 2 + core]
         return pltpu.make_async_remote_copy(
-            src_ref=block, dst_ref=block, send_sem=ssem4.at[n], recv_sem=rsem4.at[n],
+            src_ref=block, dst_ref=block, send_sem=ssem4, recv_sem=rsem4.at[back],
             device_id=(other, d), device_id_type=MESH)
 
     def products(target, late):
@@ -298,41 +294,32 @@
             return carry
         lax.fori_loop(first, until, one, 0)
 
-    gather_tables(9, 13)
-    for half in range(2):
-        for k in range(1, NZ):
-            if NEAR.index(-k % NZ) // 4 == half:
-                along_z(send2, pool.at[b], ssem2, rsem2, k, None).wait_recv()
+    gather_tables(9, 16)
+    take(pool.at[b, pl.ds(1, 7)], rsem2)
+    for way in range(2):
+        ring(way, 0).start()
+    across(0, 0).start()
+    compact(0, 0, core)
+    gather_tables(16, 18)
+    for s in range(4):
+        take(pool.at[pl.ds(0, 2)] if s < 3 else pool.at[0], rsem3.at[s])
         for way in range(2):
-            ring(way, half, True).start()
-        if half == 0:
-            gather_tables(13, 16)
-    across(0, True).start()
-    compact(0, 0, core)
-    unit = 16
-    for n, (s, h) in enumerate(slots):
-        for way in range(2):
-            ring(way, n, False).wait_recv()
-            if s < 2 or (s == 2 and h == way):
-                ring(way, n + 2 if s < 2 else 6, True).start()
-        if unit < 24:
-            gather_tables(unit, unit + 2)
-            unit += 2
-        if h == 0 and s < 3:
-            continue
-        for way in range(2):
-            across(2 * s + 1 + way, True).start()
+            if s < 3:
+                ring(way, s + 1).start()
+        for way in range(2 if s < 3 else 1):
+            across(way, s + 1).start()
         for way in range(2 if s < 3 else 1):
             compact(way, s + 1, core)
-        for m in ((0,), (1, 2), (3, 4), (5, 6))[s]:
-            across(m, False).wait_recv()
-            way, back = (0, 0) if m == 0 else ((m + 1) % 2, (m + 1) // 2)
-            compact(way, back, 1 - core)
+        if s < 2:
+            gather_tables(18 + 3 * s, 21 + 3 * s)
+        if s == 3:
+            early(4, 8)
+        take(pool.at[pl.ds(0, 2)] if s > 0 else pool.at[0], rsem4.at[s])
+        for way in range(2 if s > 0 else 1):
+            compact(way, s, 1 - core)
         if s == 2:
-            early(0, 5)
-    early(5, 8)
-    across(7, False).wait_recv()
-    across(8, False).wait_recv()
+            early(0, 4)
+    take(pool.at[0], rsem4.at[4])
     compact(0, 4, 1 - core)
 
     def one_owner(i, carry):
@@ -353,25 +340,19 @@
     back1[mine, :] = back0[mine, :]
     for load in loads[9:]:
         load.wait()
-    for k in range(1, NY):
-        along_y(back0, back1, ssem5, rsem5, k, (y + NY - k) % NY).wait_recv()
+    take(back1.at[pl.ds(0, 112)], rsem5)
     for target in range(NZ):
         for r in range(2):
             back2[target, r] = back1[pl.ds(r * 8 + target, 8, stride=16), :]
     for k in far_first:
         along_z(back2, last, ssem6, rsem6, k, z).start()
     last[z] = back2[z]
-    for k in range(1, NY):
-        along_y(send0, recv1, ssem1, rsem1, k, y).wait_send()
-        along_z(send2, pool.at[b], ssem2, rsem2, k, None).wait_send()
-        along_y(back0, back1, ssem5, rsem5, k, y).wait_send()
-    for n in range(7):
-        for way in range(2):
-            ring(way, n, True).wait_send()
-    for n in range(9):
-        across(n, True).wait_send()
-    for k in range(1, NZ):
-        along_z(back2, last, ssem6, rsem6, k, (z + NZ - k) % NZ).wait_recv()
+    take(send0.at[pl.ds(0, 112)], ssem1)
+    take(send2.at[pl.ds(0, 7)], ssem2)
+    take(pool.at[pl.ds(0, 7)], ssem3)
+    take(pool.at[pl.ds(0, 8)], ssem4)
+    take(back0.at[pl.ds(0, 112)], ssem5)
+    take(last.at[pl.ds(0, 7)], rsem6)
 
     real = last[:, 0].reshape(TP, PP)
     imag = last[:, 1].reshape(TP, PP)
@@ -392,8 +373,7 @@
         for r in range(2):
             n = o * 2 + r
             out_ref[pl.ds(o * 32 + r, 16, stride=2), :] = result[n * 16:(n + 1) * 16]
-    for k in range(1, NZ):
-        along_z(back2, last, ssem6, rsem6, k, z).wait_send()
+    take(back2.at[pl.ds(0, 7)], ssem6)
 
 
 def whole():
@@ -421,7 +401,7 @@
             vmem((GROUPS * CAP, 128), BF), vmem((2 * GROUPS * CAP, 256), BF), vmem((768, 256), BF),
             vmem((24 * 512, 256), f32),
             vmem((128, 128), f32), vmem((128, 128), f32), vmem((128, 128), f32), vmem(tile, f32), vmem(tile, f32), dma(11),
-            dma(8), dma(8), dma(8), dma(8), dma(2, 7), dma(2, 7), dma(9), dma(9), dma(8), dma(8), dma(8), dma(8)],
+            dma(), dma(), dma(), dma(), dma(), dma(4), dma(), dma(5), dma(), dma(), dma(), dma()],
         compiler_params=pltpu.CompilerParams(collective_id=0, has_side_effects=True, vmem_limit_bytes=60 << 20),
         name="level_pair",
     )(fields, table, send_rows, slots, trans, counts, *const)

time: 63.6 us -> 63.2 us (level)
  the two profiles are of different devices: /device:TPU:6 before, /device:TPU:4 now
where the time goes in v4:
time: 63.2 us; the launch traced here: 63.1 us
  Pallas kernels  61.5 us (97%)
  local copies, waits for them, and re-layouts  1.57 us (2%)
    pallas_call x1, Pallas kernels, whole_step(): pl.pallas_call(kernel, out_shape=jax.ShapeDtypeStruct((256, 128), f32), i...  61.5 us
    unnamed x1, local copies, waits for them, and re-layouts  1.57 us

profile of v4, /device:TPU:4, one launch (start us, length us, event | category | flops | bytes accessed | tf_op | source)
XLA Modules:
  0.0 63.1 jit_solution(9575452426936170102)
XLA Ops:
  0.0 61.5 %level_pair.1 = f32[256,128]{1,0:T(8,128)} custom-call(f32[256,128]{1,0:T(8,128)} %bitcast.14, f32[632,128]{1,0:T(8,128)} %bitcast.13, s32[16,16,32]{2,1,0:T(8,128)} %send_hbm.1, s32[64,189]{1,0:T(8,128)} %slot_hbm.1, s32[64,189]{1,0:T(8,128)} %trans_hbm.1, s32[1,64]{1,0:T(1,128)} %bitcast.15, bf16[384,256]{1,0:T(8,128)(2,1)} %constant.10.clone.phi_out_hbm, ...), custom_call_target="tpu_custom_call" | custom-call | tf_op jit(solution)/shard_map/level_pair/pallas_call | solution.py:391
  61.5 1.6 %copy.15 = f32[8,2,2048]{2,1,0:T(2,128)} copy(f32[8,2,2048]{2,1,0:T(2,128)} %bitcast.12) | data formatting | bytes 262144

commit v5 on v4

--- a/solution.py
+++ b/solution.py
@@ -216,7 +216,7 @@
             return carry
         lax.fori_loop(first, until, one, 0)
 
-    gather_tables(0, 9)
+    gather_tables(0, 12)
     take(recv1.at[pl.ds(0, 112)], rsem1)
     for target in range(NZ):
         for r in range(2):
@@ -294,13 +294,13 @@
             return carry
         lax.fori_loop(first, until, one, 0)
 
-    gather_tables(9, 16)
+    gather_tables(12, 22)
     take(pool.at[b, pl.ds(1, 7)], rsem2)
     for way in range(2):
         ring(way, 0).start()
     across(0, 0).start()
     compact(0, 0, core)
-    gather_tables(16, 18)
+    gather_tables(22, 24)
     for s in range(4):
         take(pool.at[pl.ds(0, 2)] if s < 3 else pool.at[0], rsem3.at[s])
         for way in range(2):
@@ -310,17 +310,16 @@
             across(way, s + 1).start()
         for way in range(2 if s < 3 else 1):
             compact(way, s + 1, core)
-        if s < 2:
-            gather_tables(18 + 3 * s, 21 + 3 * s)
-        if s == 3:
-            early(4, 8)
-        take(pool.at[pl.ds(0, 2)] if s > 0 else pool.at[0], rsem4.at[s])
-        for way in range(2 if s > 0 else 1):
-            compact(way, s, 1 - core)
-        if s == 2:
-            early(0, 4)
-    take(pool.at[0], rsem4.at[4])
-    compact(0, 4, 1 - core)
+        if s == 0:
+            take(pool.at[0], rsem4.at[0])
+            compact(0, 0, 1 - core)
+        if s > 1:
+            early(3 * s - 4, 3 * s - 1)
+        take(pool.at[pl.ds(0, 2)] if s < 3 else pool.at[0], rsem4.at[s + 1])
+        for way in range(2 if s < 3 else 1):
+            compact(way, s + 1, 1 - core)
+        if s == 1:
+            early(0, 2)
 
     def one_owner(i, carry):
         k = 4 + (i + 1) // 2 * (1 - 2 * (i % 2))

time: 63.2 us -> 63.4 us (level)
  no operation moved by 1% of the time
where the time goes in v5:
time: 63.4 us; the launch traced here: 63.3 us
  Pallas kernels  61.7 us (97%)
  local copies, waits for them, and re-layouts  1.57 us (2%)
    pallas_call x1, Pallas kernels, whole_step(): pl.pallas_call(kernel, out_shape=jax.ShapeDtypeStruct((256, 128), f32), i...  61.7 us
    unnamed x1, local copies, waits for them, and re-layouts  1.57 us

profile of v5, /device:TPU:4, one launch (start us, length us, event | category | flops | bytes accessed | tf_op | source)
XLA Modules:
  0.0 63.3 jit_solution(16499843045653759483)
XLA Ops:
  0.0 61.7 %level_pair.1 = f32[256,128]{1,0:T(8,128)} custom-call(f32[256,128]{1,0:T(8,128)} %bitcast.14, f32[632,128]{1,0:T(8,128)} %bitcast.13, s32[16,16,32]{2,1,0:T(8,128)} %send_hbm.1, s32[64,189]{1,0:T(8,128)} %slot_hbm.1, s32[64,189]{1,0:T(8,128)} %trans_hbm.1, s32[1,64]{1,0:T(1,128)} %bitcast.15, bf16[384,256]{1,0:T(8,128)(2,1)} %constant.10.clone.phi_out_hbm, ...), custom_call_target="tpu_custom_call" | custom-call | tf_op jit(solution)/shard_map/level_pair/pallas_call | solution.py:390
  61.7 1.6 %copy.15 = f32[8,2,2048]{2,1,0:T(2,128)} copy(f32[8,2,2048]{2,1,0:T(2,128)} %bitcast.12) | data formatting | bytes 262144

commit v6 on v5

--- a/solution.py
+++ b/solution.py
@@ -74,7 +74,7 @@
     back = np.zeros((256, 128))
     back[:128, :64] = phi
     back[128:, 64:] = phi
-    high, low = halves(back * (TC * PC / (TP * PP)))
+    high, low = halves(back)
     phi_in = np.concatenate([high, high, low], axis=0)
     tables = np.concatenate([cosines[:4].reshape(256, 128), sines[:4].reshape(256, 128)]).astype(np.float32)
     return phi_out, theta_out, tables, theta_in, phi_in
@@ -314,12 +314,12 @@
             take(pool.at[0], rsem4.at[0])
             compact(0, 0, 1 - core)
         if s > 1:
-            early(3 * s - 4, 3 * s - 1)
+            early(3 if s == 2 else 7, 7 if s == 2 else 8)
         take(pool.at[pl.ds(0, 2)] if s < 3 else pool.at[0], rsem4.at[s + 1])
         for way in range(2 if s < 3 else 1):
             compact(way, s + 1, 1 - core)
         if s == 1:
-            early(0, 2)
+            early(0, 3)
 
     def one_owner(i, carry):
         k = 4 + (i + 1) // 2 * (1 - 2 * (i % 2))
@@ -410,7 +410,7 @@
     fields = child_outgoing.reshape(8, 2, 16, 128).transpose(0, 2, 1, 3).reshape(256, 128)
     out = whole_step(fields, trans_table.reshape(NTRANS * 2, 128), send_rows, far_slot, far_trans,
                      far_count.reshape(1, 64), const)
-    return out.reshape(8, 16, 2, 128).transpose(0, 2, 1, 3).reshape(8, 2, 2048)
+    return out.reshape(8, 16, 2, 128).transpose(0, 2, 1, 3).reshape(8, 2, 2048) * (TC * PC / (TP * PP))
 
 
 def solution(mesh):

time: 63.4 us -> 62.1 us (0.979)
  other arithmetic: 0 us -> 1.57 us
  local copies, waits for them, and re-layouts: 1.57 us -> 0 us
  Pallas kernels: 61.7 us -> 60.4 us
    mul x0 -> x1, other arithmetic: none -> 1.57 us  [on_device(): out.reshape(8, 16, 2, 128).transpose(0, 2, 1, 3).reshape(8, 2, 2048)]
    unnamed x1 -> x0, local copies, waits for them, and re-layouts: 1.57 us -> none
    pallas_call x1, Pallas kernels: 61.7 us -> 60.4 us  [whole_step(): pl.pallas_call(kernel, out_shape=jax.ShapeDtypeStruct((256, 128), f32), i...]
where the time goes in v6:
time: 62.1 us; the launch traced here: 61.9 us
  Pallas kernels  60.4 us (97%)
  other arithmetic  1.57 us (3%)
    pallas_call x1, Pallas kernels, whole_step(): pl.pallas_call(kernel, out_shape=jax.ShapeDtypeStruct((256, 128), f32), i...  60.4 us
    mul x1, other arithmetic, on_device(): out.reshape(8, 16, 2, 128).transpose(0, 2, 1, 3).reshape(8, 2, 2048)  1.57 us

profile of v6, /device:TPU:4, one launch (start us, length us, event | category | flops | bytes accessed | tf_op | source)
XLA Modules:
  0.0 61.9 jit_solution(10385616415714717556)
XLA Ops:
  0.0 60.4 %level_pair.1 = f32[256,128]{1,0:T(8,128)} custom-call(f32[256,128]{1,0:T(8,128)} %bitcast.13, f32[632,128]{1,0:T(8,128)} %bitcast.12, s32[16,16,32]{2,1,0:T(8,128)} %send_hbm.1, s32[64,189]{1,0:T(8,128)} %slot_hbm.1, s32[64,189]{1,0:T(8,128)} %trans_hbm.1, s32[1,64]{1,0:T(1,128)} %bitcast.14, bf16[384,256]{1,0:T(8,128)(2,1)} %constant.12.clone.phi_out_hbm, ...), custom_call_target="tpu_custom_call" | custom-call | tf_op jit(solution)/shard_map/level_pair/pallas_call | solution.py:390
  60.4 1.6 %broadcast_multiply_fusion = f32[256,128]{1,0:T(8,128)} fusion(f32[256,128]{1,0:T(8,128)} %level_pair.1), kind=kLoop, calls=%fused_computation | loop fusion | flops 32768 | bytes 262144 | tf_op jit(solution)/shard_map/mul | solution.py:413
